TPU v7x, 512 devices: a whole 4x4x16 slice. The times are simulated.
512 devices in a mesh: seq: 32 (over y, x, core), mp: 16 (over z).
Axes of the slice: x: 4, y: 4, z: 16, core: 2. Of those that a mesh axis runs over, the one named last changes fastest.
Arguments:
- enc_states: bfloat16 [98304, 1280], P(('seq', 'mp')), may hold values from -6 to 6
- dec_states: bfloat16 [98304, 1280], P(('seq', 'mp')), may hold values from -240 to 240
- segments: int32 [98304], P(('seq', 'mp')), may hold values from 0 to 30, as said below
- patch_keys: bfloat16 [15872, 1280], P(('seq', 'mp')), may hold values from -7 to 7
- w_in: bfloat16 [1280, 4096], P(None, 'mp'), may hold values from -0.15625 to 0.15625
- w_gate: bfloat16 [4096, 7168], P('seq', 'mp'), may hold values from -0.09375 to 0.09375
- w_up: bfloat16 [4096, 7168], P('seq', 'mp'), may hold values from -0.09375 to 0.09375
- w_down: bfloat16 [7168, 4096], P('mp', 'seq'), may hold values from -0.0625 to 0.0625
- w_out: bfloat16 [4096, 1280], P('mp'), may hold values from -0.09375 to 0.09375
Outputs:
- decoded: bfloat16 [98304, 1280], P(('seq', 'mp'))
Inputs may be any that keep to these rules, and one draw needn't show every extreme that they name: `segments`: within each block of 192 bytes the patch number starts at 0 and rises by 0 or 1 from byte to byte. Block b belongs to device b, counted seq first; the blocks of the devices that share an mp index hold 512 patches together. A block holds at most 31 patches, and in every such set of blocks one holds exactly 31.
All inputs are finite; a program needn't handle non-finite values.
Results may differ from a plain program's by a relative error of at most 0.01.
Values may be sent and summed in bfloat16 or wider, within the bound.
A program may use at most 64 MiB of HBM per device.

v0:
```python
import math

import jax
import jax.numpy as jnp
from jax import lax
from jax.sharding import PartitionSpec as P

HD = 128
RMEAN = 16


norm_epsilon = 1e-05


def copy_for_each(value, axis):
    peers = lax.axis_size(axis)
    return lax.all_to_all(
        jnp.broadcast_to(value[None], (peers, *value.shape)), axis, 0, 0, tiled=True
    )


def in_order(blocks, dim):
    blocks = jnp.moveaxis(blocks, 0, dim)
    lengths = blocks.shape
    return blocks.reshape(*lengths[:dim], lengths[dim] * lengths[dim + 1], *lengths[dim + 2 :])


def collect(value, axis, dim):
    blocks = copy_for_each(value, axis)
    return in_order(blocks, dim)


def in_one_piece(arrays, axis, dim, along):
    widths = [a.shape[along] for a in arrays]
    both = jnp.concatenate(arrays, axis=along)
    whole = lax.all_gather(both, axis, axis=dim, tiled=True)
    return tuple(jnp.split(whole, [sum(widths[:k]) for k in range(1, len(widths))], axis=along))


def in_blocks(value, dim, peers):
    before, after = (value.shape[:dim], value.shape[dim + 1 :])
    return jnp.moveaxis(value.reshape(*before, peers, -1, *after), dim, 0)


def sum_at_owner(value, axis, dim):
    peers = lax.axis_size(axis)
    blocks = lax.all_to_all(in_blocks(value, dim, peers), axis, 0, 0, tiled=True)
    return jnp.sum(blocks.astype(jnp.float32), axis=0)


def body(enc_states, dec_states, segments, patch_keys, w_in, w_gate, w_up, w_down, w_out):
    byte_rows = segments.shape[0]
    most_patches = patch_keys.shape[0]
    width = enc_states.shape[1]
    seq_size = lax.axis_size("seq")
    slots = -(-most_patches // seq_size)
    local_ids = jnp.arange(most_patches, dtype=jnp.int32)
    member = segments[None, :] == local_ids[:, None]
    pool_sums = jnp.dot(member.astype(jnp.bfloat16), enc_states, preferred_element_type=jnp.float32)
    lengths = jnp.sum(member.astype(jnp.float32), axis=1)
    pooled = (pool_sums / jnp.maximum(lengths, 1.0)[:, None]).astype(jnp.bfloat16)
    patch_total = segments[byte_rows - 1] + 1
    all_counts = collect(patch_total.reshape(1), "seq", 0)
    my_index = lax.axis_index("seq")
    source_ids = jnp.arange(seq_size, dtype=jnp.int32)
    starts = jnp.cumsum(all_counts) - all_counts
    my_start = jnp.sum(jnp.where(source_ids == my_index, starts, 0))
    owner_ids = jnp.arange(seq_size * slots, dtype=jnp.int32) // slots
    slot_ids = jnp.arange(seq_size * slots, dtype=jnp.int32) % slots
    send_patch = jnp.mod(owner_ids - my_start, seq_size) + slot_ids * seq_size
    send_live = send_patch < patch_total
    picker = ((send_patch[:, None] == local_ids[None, :]) & send_live[:, None]).astype(jnp.bfloat16)
    outgoing = jnp.dot(picker, pooled, preferred_element_type=jnp.float32).astype(jnp.bfloat16)
    incoming = lax.all_to_all(
        outgoing.reshape(seq_size, slots, width), "seq", split_axis=0, concat_axis=0, tiled=True
    )
    source_start = jnp.repeat(starts, slots)
    source_total = jnp.repeat(all_counts, slots)
    recv_patch = jnp.mod(my_index - source_start, seq_size) + slot_ids * seq_size
    recv_live = recv_patch < source_total
    recv_place = (source_start + recv_patch) // seq_size
    owned_ids = jnp.arange(RMEAN, dtype=jnp.int32)
    placer = ((recv_place[None, :] == owned_ids[:, None]) & recv_live[None, :]).astype(jnp.bfloat16)
    owned = jnp.dot(
        placer, incoming.reshape(seq_size * slots, width), preferred_element_type=jnp.float32
    ).astype(jnp.bfloat16)
    x_part = jnp.dot(collect(owned, "mp", 0), w_in, preferred_element_type=jnp.float32).astype(
        jnp.bfloat16
    )
    x_full = collect(x_part, "mp", 1)
    x_wide = x_full.astype(jnp.float32)
    square_mean = jnp.mean(x_wide * x_wide, axis=1, keepdims=True)
    normed = (x_wide * lax.rsqrt(square_mean + norm_epsilon)).astype(jnp.bfloat16)
    pieces = in_one_piece((w_gate, w_up), "seq", 0, 1)
    gate_next = jnp.dot(normed, pieces[0], preferred_element_type=jnp.float32)
    up_next = jnp.dot(normed, pieces[1], preferred_element_type=jnp.float32)
    hidden = (jax.nn.silu(gate_next) * up_next).astype(jnp.bfloat16)
    down_terms = jnp.dot(
        hidden,
        lax.all_gather(w_down, "seq", axis=1, tiled=True),
        preferred_element_type=jnp.float32,
    )
    down_part = sum_at_owner(down_terms.astype(jnp.bfloat16), "mp", 1)
    residual = (x_part.astype(jnp.float32) + down_part).astype(jnp.bfloat16)
    outputs = sum_at_owner(
        jnp.dot(residual, w_out, preferred_element_type=jnp.float32).astype(jnp.bfloat16), "mp", 0
    ).astype(jnp.bfloat16)
    backward = jnp.dot(jnp.transpose(placer), outputs, preferred_element_type=jnp.float32).astype(
        jnp.bfloat16
    )
    returned = lax.all_to_all(
        backward.reshape(seq_size, slots, width), "seq", split_axis=0, concat_axis=0, tiled=True
    )
    patch_values = jnp.dot(
        jnp.transpose(picker),
        returned.reshape(seq_size * slots, width),
        preferred_element_type=jnp.float32,
    ).astype(jnp.bfloat16)
    heads = width // HD
    queries = dec_states.reshape(byte_rows, heads, HD)
    keys_local = patch_keys.reshape(most_patches, heads, HD)
    values_local = patch_values.reshape(most_patches, heads, HD)
    scores = jnp.einsum(
        "bhd,jhd->hbj", queries, keys_local, preferred_element_type=jnp.float32
    ) / math.sqrt(HD)
    allowed = local_ids[None, :] <= segments[:, None]
    scores = jnp.where(allowed[None, :, :], scores, -1e30)
    peak = jnp.max(scores, axis=2, keepdims=True)
    expon = jnp.exp(scores - peak)
    weights = (expon / jnp.sum(expon, axis=2, keepdims=True)).astype(jnp.bfloat16)
    mixed = jnp.einsum("hbj,jhd->bhd", weights, values_local, preferred_element_type=jnp.float32)
    return (dec_states.astype(jnp.float32) + mixed.reshape(byte_rows, width)).astype(jnp.bfloat16)


def solution(mesh):
    placed = (
        P(("seq", "mp"), None),
        P(("seq", "mp"), None),
        P(("seq", "mp")),
        P(("seq", "mp"), None),
        P(None, "mp"),
        P("seq", "mp"),
        P("seq", "mp"),
        P("mp", "seq"),
        P("mp", None),
    )
    return jax.shard_map(
        body, mesh=mesh, in_specs=placed, out_specs=P(("seq", "mp"), None), check_vma=False
    )
```

profile of v0, /device:TPU:6, one launch (start us, length us, event | category | flops | bytes accessed | tf_op | source)
XLA Modules:
  0.0 380.6 jit_solution(12821737070578798660)
XLA Ops:
  6.5 1.8 pad_maximum_fusion
  8.3 1.3 slice.3
  10.2 0.6 broadcast_in_dim.16
  10.8 9.4 %all-to-all-start = ((s32[32,1,1]{2,1,0:T(1,128)}), s32[32,1,1]{2,1,0:T(1,128)S(1)}, u32[]{:S(2)}, u32[]{:S(2)}) async-start(s32[32,1,1]{2,1,0:T(1,128)} %broadcast_in_dim.16), calls=%async_computation | async-start | bytes 32768 | tf_op jit(solution)/shard_map/all_to_all | solution.py:17
  20.2 0.8 convert_reduce_fusion.1
  21.0 4.8 %all-to-all-done = s32[32,1,1]{2,1,0:T(1,128)S(1)} async-done(((s32[32,1,1]{2,1,0:T(1,128)}), s32[32,1,1]{2,1,0:T(1,128)S(1)}, u32[]{:S(2)}, u32[]{:S(2)}) %all-to-all-start) | async-done | bytes 160 | tf_op jit(solution)/shard_map/all_to_all | solution.py:17
  25.8 0.1 reduce.3
  25.9 0.7 reduce.4
  26.6 0.7 and_select_fusion
  27.4 0.7 broadcast_compare_fusion
  28.1 0.7 and_select_fusion.2
  28.8 1.4 fusion.7
  30.1 0.6 broadcast.286
  30.7 0.6 reduce.5
  31.4 11.3 %all_to_all.36 = bf16[32,2,640]{2,1,0:T(2,128)(2,1)S(1)} all-to-all(bf16[32,2,640]{2,1,0:T(2,128)(2,1)S(1)} %reshape.182), channel_id=1, replica_groups=mesh['seq'=32,'mp'=16] {'seq'}, dimensions={0} | all-to-all | bytes 163840 | tf_op jit(solution)/shard_map/all_to_all | solution.py:74
  42.7 0.1 convolution_convert_fusion.5
  42.9 49.6 %all_to_all.37 = bf16[16,16,1280]{2,1,0:T(8,128)(2,1)S(1)} all-to-all(bf16[16,16,1280]{2,1,0:T(8,128)(2,1)S(1)} %broadcast_in_dim.17), channel_id=1, replica_groups=mesh['seq'=32,'mp'=16] {'mp'}, dimensions={0} | all-to-all | bytes 1310720 | tf_op jit(solution)/shard_map/all_to_all | solution.py:17
  92.6 0.3 convolution_convert_fusion.6
  92.9 0.1 copy.61
  93.0 1.6 broadcast_in_dim.18
  94.6 4.4 %all-to-all-start.3 = ((bf16[16,256,256]{1,2,0:T(8,128)(2,1)}), bf16[16,256,256]{1,2,0:T(8,128)(2,1)S(1)}, u32[]{:S(2)}, u32[]{:S(2)}) async-start(bf16[16,256,256]{1,2,0:T(8,128)(2,1)} %broadcast_in_dim.18), calls=%async_computation.3 | async-start | bytes 4194304 | tf_op jit(solution)/shard_map/all_to_all | solution.py:17
  99.1 0.7 all-gather.5.cloned.1.call-update
  99.8 94.5 %all-to-all-done.3 = bf16[16,256,256]{1,2,0:T(8,128)(2,1)S(1)} async-done(((bf16[16,256,256]{1,2,0:T(8,128)(2,1)}), bf16[16,256,256]{1,2,0:T(8,128)(2,1)S(1)}, u32[]{:S(2)}, u32[]{:S(2)}) %all-to-all-start.3) | async-done | bytes 2097184 | tf_op jit(solution)/shard_map/all_to_all | solution.py:17
  194.3 0.6 multiply_reduce_fusion
  194.9 1.8 fusion.1
  196.7 4.0 %fusion.4 = f32[256,448]{0,1:T(8,128)S(1)} fusion(bf16[256,4096]{0,1:T(8,128)(2,1)} %fusion.1, bf16[4096,896]{0,1:T(8,128)(2,1)} %all-gather.3.cloned.1.call-done), kind=kOutput, calls=%fused_computation.8 | convolution fusion | flops 939524096 | bytes 6225920 | tf_op jit(solution)/shard_map/dot_general | solution.py:95
  200.7 8.7 %convolution_convert_fusion = bf16[256,4096]{1,0:T(8,128)(2,1)} fusion(bf16[448,4096]{1,0:T(8,128)(2,1)} %all-gather.5.cloned.1.call-done, bf16[256,4096]{0,1:T(8,128)(2,1)S(1)} %copy-done.1, bf16[4096,896]{0,1:T(8,128)(2,1)} %all-gather.3.cloned.1.call-done, f32[256,448]{0,1:T(8,128)S(1)} %fusion.4), kind=kOutput, calls=%fused_computation.1 | convolution fusion | flops 1880784896 | bytes 11993088 | tf_op jit(solution)/shard_map/dot_general | solution.py:98
  209.4 1.8 copy.87
  211.2 104.2 %all_to_all.38 = bf16[16,256,256]{2,1,0:T(8,128)(2,1)S(1)} all-to-all(bf16[16,256,256]{2,1,0:T(8,128)(2,1)S(1)} %bitcast.42), channel_id=1, replica_groups=mesh['seq'=32,'mp'=16] {'mp'}, dimensions={0} | all-to-all | bytes 4194304 | tf_op jit(solution)/shard_map/all_to_all | solution.py:47
  315.4 0.3 convert_reduce_fusion
  315.7 1.2 convolution_convert_fusion.1
  316.9 6.3 %all-to-all-start.5 = ((bf16[16,16,1280]{2,1,0:T(8,128)(2,1)}), bf16[16,16,1280]{2,1,0:T(8,128)(2,1)S(1)}, u32[]{:S(2)}, u32[]{:S(2)}) async-start(bf16[16,16,1280]{2,1,0:T(8,128)(2,1)} %bitcast.7), calls=%async_computation.5 | async-start | bytes 1310720 | tf_op jit(solution)/shard_map/all_to_all | solution.py:47
  323.2 0.2 copy.64
  323.5 0.1 reshape.177
  323.6 0.2 fusion.17
  323.8 33.4 %all-to-all-done.5 = bf16[16,16,1280]{2,1,0:T(8,128)(2,1)S(1)} async-done(((bf16[16,16,1280]{2,1,0:T(8,128)(2,1)}), bf16[16,16,1280]{2,1,0:T(8,128)(2,1)S(1)}, u32[]{:S(2)}, u32[]{:S(2)}) %all-to-all-start.5) | async-done | bytes 655392 | tf_op jit(solution)/shard_map/all_to_all | solution.py:47
  357.2 0.1 reduce_sum.61
  357.3 0.2 fusion.8
  357.5 0.6 reduce.6
  358.1 0.6 reshape.184
  358.8 5.6 %all-to-all-start.6 = ((bf16[32,2,640]{2,1,0:T(2,128)(2,1)}), bf16[32,2,640]{2,1,0:T(2,128)(2,1)S(1)}, u32[]{:S(2)}, u32[]{:S(2)}) async-start(bf16[32,2,640]{2,1,0:T(2,128)(2,1)} %reshape.184), calls=%async_computation.6 | async-start | bytes 163840 | tf_op jit(solution)/shard_map/all_to_all | solution.py:111
  364.4 0.1 fusion.56
  364.5 5.7 %all-to-all-done.6 = bf16[32,2,640]{2,1,0:T(2,128)(2,1)S(1)} async-done(((bf16[32,2,640]{2,1,0:T(2,128)(2,1)}), bf16[32,2,640]{2,1,0:T(2,128)(2,1)S(1)}, u32[]{:S(2)}, u32[]{:S(2)}) %all-to-all-start.6) | async-done | bytes 81952 | tf_op jit(solution)/shard_map/all_to_all | solution.py:111
  370.3 0.3 convolution_convert_fusion.2
  370.6 1.5 convolution_bitcast_fusion
  372.1 0.4 copy.68
  372.5 0.4 copy.69
  372.9 0.9 add_convert_fusion
  (29 shorter events, 0.5 us)
Async XLA Ops:
  6.5 309.2 %copy-start = (bf16[256,1280]{1,0:T(8,128)(2,1)S(1)}, bf16[256,1280]{1,0:T(8,128)(2,1)}, u32[]{:S(2)}) copy-start(bf16[256,1280]{1,0:T(8,128)(2,1)} %param.17) | copy-start | bytes 1966084
  6.5 86.0 %copy-start.3 = (bf16[1280,256]{1,0:T(8,128)(2,1)S(1)}, bf16[1280,256]{1,0:T(8,128)(2,1)}, u32[]{:S(2)}) copy-start(bf16[1280,256]{1,0:T(8,128)(2,1)} %param.13) | copy-start | bytes 1966084
  6.5 190.1 %all-gather.3.cloned.1.call-start = ((), (), s32[]{:S(2)}) async-start(), calls=%async_computation.7 | async-start | bytes 7569408 | tf_op jit(solution)/shard_map/all_gather | solution.py:36
  10.8 15.0 %all-to-all-start = ((s32[32,1,1]{2,1,0:T(1,128)}), s32[32,1,1]{2,1,0:T(1,128)S(1)}, u32[]{:S(2)}, u32[]{:S(2)}) async-start(s32[32,1,1]{2,1,0:T(1,128)} %broadcast_in_dim.16), calls=%async_computation | async-start | bytes 32768 | tf_op jit(solution)/shard_map/all_to_all | solution.py:17
  94.6 99.7 %all-to-all-start.3 = ((bf16[16,256,256]{1,2,0:T(8,128)(2,1)}), bf16[16,256,256]{1,2,0:T(8,128)(2,1)S(1)}, u32[]{:S(2)}, u32[]{:S(2)}) async-start(bf16[16,256,256]{1,2,0:T(8,128)(2,1)} %broadcast_in_dim.18), calls=%async_computation.3 | async-start | bytes 4194304 | tf_op jit(solution)/shard_map/all_to_all | solution.py:17
  99.0 101.7 %all-gather.5.cloned.1.call-start = ((), (), s32[]{:S(2)}) async-start(), calls=%async_computation.8 | async-start | bytes 3784704 | tf_op jit(solution)/shard_map/all_gather | solution.py:100
  196.7 4.0 %copy-start.1 = (bf16[256,4096]{0,1:T(8,128)(2,1)S(1)}, bf16[256,4096]{0,1:T(8,128)(2,1)}, u32[]{:S(2)}) copy-start(bf16[256,4096]{0,1:T(8,128)(2,1)} %fusion.1) | copy-start | bytes 6291460
  315.4 7.8 %copy-start.2 = (bf16[192,1280]{1,0:T(8,128)(2,1)S(1)}, bf16[192,1280]{1,0:T(8,128)(2,1)}, u32[]{:S(2)}) copy-start(bf16[192,1280]{1,0:T(8,128)(2,1)} %param.10) | copy-start | bytes 1474564
  315.4 8.0 %copy-start.5 = (bf16[31,1280]{1,0:T(8,128)(2,1)S(1)}, bf16[31,1280]{1,0:T(8,128)(2,1)}, u32[]{:S(2)}) copy-start(bf16[31,1280]{1,0:T(8,128)(2,1)} %param.12) | copy-start | bytes 238084
  315.4 8.1 %copy-start.6 = (s32[192]{0:T(256)S(1)}, s32[192]{0:T(256)}, u32[]{:S(2)}) copy-start(s32[192]{0:T(256)} %param.11) | copy-start | bytes 2308
  316.9 40.3 %all-to-all-start.5 = ((bf16[16,16,1280]{2,1,0:T(8,128)(2,1)}), bf16[16,16,1280]{2,1,0:T(8,128)(2,1)S(1)}, u32[]{:S(2)}, u32[]{:S(2)}) async-start(bf16[16,16,1280]{2,1,0:T(8,128)(2,1)} %bitcast.7), calls=%async_computation.5 | async-start | bytes 1310720 | tf_op jit(solution)/shard_map/all_to_all | solution.py:47
  323.8 46.7 %copy-start.4 = (f32[10,192,31]{1,2,0:T(8,128)}, f32[10,192,31]{1,2,0:T(8,128)S(1)}, u32[]{:S(2)}) copy-start(f32[10,192,31]{1,2,0:T(8,128)S(1)} %fusion.17) | copy-start | bytes 714244
  358.8 11.4 %all-to-all-start.6 = ((bf16[32,2,640]{2,1,0:T(2,128)(2,1)}), bf16[32,2,640]{2,1,0:T(2,128)(2,1)S(1)}, u32[]{:S(2)}, u32[]{:S(2)}) async-start(bf16[32,2,640]{2,1,0:T(2,128)(2,1)} %reshape.184), calls=%async_computation.6 | async-start | bytes 163840 | tf_op jit(solution)/shard_map/all_to_all | solution.py:111
Sparse Core Ops, SparseCore 0:
  10.4 75.7 all-gather.2
  102.9 61.2 all-gather.4
where the time goes:
time: 384 us; the launch traced here: 381 us
  blocking collectives  165 us (43%)
  waiting for transfers between devices  139 us (36%)
  starting transfers between devices  25.7 us (7%)
  matrix products  17.9 us (5%)
  between operations  14.2 us (4%)
  other arithmetic  10.5 us (3%)
  local copies, waits for them, and re-layouts  7.94 us (2%)
    all_to_all x1, blocking collectives, sum_at_owner(): lax.all_to_all(in_blocks(value, dim, peers), axis, 0, 0, tiled=True)  104 us
    all_to_all x2, waiting for transfers between devices, copy_for_each(): lax.all_to_all(jnp.broadcast_to(value[None], (peers, *value.shape)), axis...  99.3 us
    all_to_all x1, blocking collectives, copy_for_each(): lax.all_to_all(jnp.broadcast_to(value[None], (peers, *value.shape)), axis...  49.6 us
    all_to_all x1, waiting for transfers between devices, sum_at_owner(): lax.all_to_all(in_blocks(value, dim, peers), axis, 0, 0, tiled=True)  33.4 us
    all_to_all x2, starting transfers between devices, copy_for_each(): lax.all_to_all(jnp.broadcast_to(value[None], (peers, *value.shape)), axis...  13.8 us
    all_to_all x1, blocking collectives, body(): lax.all_to_all(outgoing.reshape(seq_size, slots, width), 'seq', split_axi...  11.3 us
    dot_general x1, matrix products, body(): jnp.dot(hidden, lax.all_gather(w_down, 'seq', axis=1, tiled=True), prefer...  8.72 us
  transfers between devices with their start and end apart: 6, of which 4 were waited for; matrix products, arithmetic and copies ran while one was open for 5% of the time, Pallas kernels for 0%

commit v1 on v0

v1 whole, which is shorter than its diff:
```python
import functools
import math

import jax
import jax.numpy as jnp
from jax import lax
from jax.experimental import pallas as pl
from jax.experimental.pallas import tpu as pltpu
from jax.sharding import PartitionSpec as P

MESH = pl.DeviceIdType.MESH
HD = 128
SIDE = 4
NZ = 16
SLOTS = 32
BF = jnp.bfloat16
F32 = jnp.float32
EPS = 1e-05
NT = (((1,), (1,)), ((), ()))
UP_HOPS = 8
DOWN_HOPS = 7


def mm(a, b):
    return jnp.dot(a, b, preferred_element_type=F32)


def mm_nt(a, b):
    return lax.dot_general(a, b, NT, preferred_element_type=F32)


def kernel(
    enc_ref, dec_ref, seg_ref, keys_ref, win_ref, wg_ref, wu_ref, wd_ref, wout_ref,
    out_ref,
    rg, ru, rd, bc, ua, rsb, wf, pall, xo, st, ob, rzp, szp, rzm, szm, kpad, wts,
    raw_s, raw_r, loc_s, bc_r, bc_sp, bc_sm, rs_s, rs_r, w_s, w_r,
    p_r, p_sp, p_sm, st_r, st_sp, st_sm, zp_s, zp_r, zm_s, zm_r,
):
    s = lax.axis_index("seq")
    z = lax.axis_index("mp")
    k = s % 2
    x = (s // 2) % SIDE
    y = s // (2 * SIDE)
    a = x + k * (y - x)
    b = y + k * (x - y)
    width = enc_ref.shape[1]
    half = width // 2
    quarter = half // SIDE
    units = wg_ref.shape[1]
    pad = 512
    lanes = 3 * pad // SIDE
    depth = wg_ref.shape[0]

    def dev(xx, yy, kk, zz):
        return {"seq": (yy * SIDE + xx) * 2 + kk, "mp": zz}

    def x_peer(j, kk):
        return dev((x + j) % SIDE, y, kk, z)

    def y_peer(j, kk):
        return dev(x, (y + j) % SIDE, kk, z)

    def a_peer(j):
        return dev((x + j * (1 - k)) % SIDE, (y + j * k) % SIDE, k, z)

    def b_peer(j):
        return dev((x + j * k) % SIDE, (y + j * (1 - k)) % SIDE, k, z)

    partner = dev(x, y, 1 - k, z)
    above = dev(x, y, k, (z + 1) % NZ)
    below = dev(x, y, k, (z + NZ - 1) % NZ)

    barrier = pltpu.get_barrier_semaphore()
    greeted = [partner, above, below]
    for j in (1, 2, 3):
        for kk in (0, 1):
            greeted += [x_peer(j, kk), y_peer(j, kk)]
    for d in greeted:
        pl.semaphore_signal(barrier, inc=1, device_id=d, device_id_type=MESH)
    pl.semaphore_wait(barrier, len(greeted))

    def remote(src, dst, ssem, rsem, d):
        return pltpu.make_async_remote_copy(
            src_ref=src, dst_ref=dst, send_sem=ssem, recv_sem=rsem, device_id=d, device_id_type=MESH
        )

    raws = ((wg_ref, rg), (wu_ref, ru), (wd_ref, rd))
    raw_targets = [(partner, b)]
    raw_targets += [(x_peer(j, 0), x) for j in (1, 2, 3)]
    raw_targets += [(y_peer(j, 1), y) for j in (1, 2, 3)]
    raw_sends = []
    for n, (d, slot) in enumerate(raw_targets):
        for i, (src, dst) in enumerate(raws):
            c = remote(src, dst.at[slot, k], raw_s.at[n, i], raw_r.at[slot, k, i], d)
            c.start()
            raw_sends.append(c)
    raw_local = []
    for i, (src, dst) in enumerate(raws):
        c = pltpu.make_async_copy(src, dst.at[a, k], loc_s.at[i])
        c.start()
        raw_local.append(c)

    def source(zz):
        hit0 = (zz // SIDE) == y
        hit1 = (zz % SIDE) == x
        hit = jnp.where(k == 0, hit0, hit1)
        slot = jnp.where(k == 0, zz % SIDE, zz // SIDE)
        return hit, slot

    first_row = k * half + a * quarter

    def bc_send(slot, part, up):
        sems = bc_sp if up else bc_sm
        return remote(
            bc.at[slot, part], bc.at[slot, part], sems.at[slot, part], bc_r.at[slot, part],
            above if up else below,
        )

    hit_me, slot_me = source(z)

    @pl.when(hit_me)
    def _():
        bc[slot_me, 0] = win_ref[pl.ds(pl.multiple_of(first_row, 32), quarter), :]
        bc_send(slot_me, 0, True).start()
        bc_send(slot_me, 0, False).start()
        rows = lax.broadcasted_iota(jnp.int32, (quarter, width), 0) + first_row
        cols = lax.broadcasted_iota(jnp.int32, (quarter, width), 1)
        pick = jnp.where(rows == cols, 1.0, 0.0).astype(BF)
        bc[slot_me, 1] = mm_nt(pick, wout_ref[...]).astype(BF)
        bc_send(slot_me, 1, True).start()
        bc_send(slot_me, 1, False).start()

    def bc_step(t):
        hit_u, slot_u = source((z + NZ - t) % NZ)
        hit_d, slot_d = source((z + t) % NZ)
        for part in (0, 1):

            @pl.when(hit_u)
            def _():
                bc_send(slot_u, part, True).wait_recv()
                if t < UP_HOPS:
                    bc_send(slot_u, part, True).start()

            if t <= DOWN_HOPS:

                @pl.when(hit_d)
                def _():
                    bc_send(slot_d, part, False).wait_recv()
                    if t < DOWN_HOPS:
                        bc_send(slot_d, part, False).start()

    member = lax.broadcasted_iota(jnp.int32, (SLOTS, enc_ref.shape[0]), 0) == seg_ref[...]
    member = jnp.where(member, 1.0, 0.0)
    lengths = jnp.maximum(jnp.sum(member, axis=1, keepdims=True), 1.0)
    pall[z] = (mm(member.astype(BF), enc_ref[...]) / lengths).astype(BF)

    def ring_send(buf, slot, ssem, rsem, d):
        return remote(buf.at[slot], buf.at[slot], ssem.at[slot], rsem.at[slot], d)

    def ring_step(buf, sp, sm, r, t):
        if t == 0:
            ring_send(buf, z, sp, r, above).start()
            ring_send(buf, z, sm, r, below).start()
            return
        up_slot = (z + NZ - t) % NZ
        down_slot = (z + t) % NZ
        ring_send(buf, up_slot, sp, r, above).wait_recv()
        if t < UP_HOPS:
            ring_send(buf, up_slot, sp, r, above).start()
        if t <= DOWN_HOPS:
            ring_send(buf, down_slot, sm, r, below).wait_recv()
            if t < DOWN_HOPS:
                ring_send(buf, down_slot, sm, r, below).start()

    def ring_drain(buf, sp, sm, r):
        for t in range(UP_HOPS):
            ring_send(buf, (z + NZ - t) % NZ, sp, r, above).wait_send()
        for t in range(DOWN_HOPS):
            ring_send(buf, (z + t) % NZ, sm, r, below).wait_send()

    p_step = functools.partial(ring_step, pall, p_sp, p_sm, p_r)
    st_step = functools.partial(ring_step, st, st_sp, st_sm, st_r)

    ua[...] = jnp.zeros_like(ua)
    lag = 3
    for t in range(1, UP_HOPS + 1):
        bc_step(t)
        if t >= lag:
            p_step(t - lag)

    for c in raw_local:
        c.wait()
    for n, d in enumerate(range(SIDE)):
        for kk in (0, 1):
            for i, (src, dst) in enumerate(raws):

                @pl.when(jnp.logical_or(a != d, k != kk))
                def _():
                    remote(src, dst.at[d, kk], raw_s.at[0, 0], raw_r.at[d, kk, i], partner).wait_recv()

    acc_g = jnp.zeros((quarter, units), F32)
    acc_u = jnp.zeros((quarter, units), F32)
    acc_d = jnp.zeros((quarter, units), F32)
    for i in range(SIDE):
        for kk in (0, 1):
            ins = bc[i, 0][:, kk * depth : (kk + 1) * depth]
            outs = bc[i, 1][:, kk * depth : (kk + 1) * depth]
            acc_g += mm(ins, rg[i, kk])
            acc_u += mm(ins, ru[i, kk])
            acc_d += mm_nt(outs, rd[i, kk])
    ua[:, 0:units] = acc_g.astype(BF)
    ua[:, pad : pad + units] = acc_u.astype(BF)
    ua[:, 2 * pad : 2 * pad + units] = acc_d.astype(BF)

    def piece(bb):
        return pl.ds(pl.multiple_of(bb * lanes, 128), lanes)

    rs_copies = []
    for j in (1, 2, 3):
        c = remote(ua.at[:, piece((b + j) % SIDE)], rsb.at[j - 1], rs_s.at[j - 1], rs_r.at[j - 1], b_peer(j))
        c.start()
        rs_copies.append(c)

    p_step(UP_HOPS - lag + 1)

    def place(kk, aa, bb):
        row = pl.multiple_of(kk * half + aa * quarter, 32)
        return wf.at[pl.ds(row, quarter), piece(bb)]

    w_copies = []

    def w_send(kk, aa, bb, d):
        n = len(w_copies)
        c = remote(place(kk, aa, bb), place(kk, aa, bb), w_s.at[n], w_r.at[kk, aa, bb], d)
        c.start()
        w_copies.append(c)

    def w_wait(kk, aa, bb):
        remote(place(kk, aa, bb), place(kk, aa, bb), w_s.at[0], w_r.at[kk, aa, bb], partner).wait_recv()

    total = ua[:, piece(b)].astype(F32)
    for c in rs_copies:
        c.wait_recv()
    for j in (0, 1, 2):
        total += rsb[j].astype(F32)
    wf[pl.ds(pl.multiple_of(first_row, 32), quarter), piece(b)] = total.astype(BF)
    for j in (1, 2, 3):
        w_send(k, a, b, b_peer(j))
    for j in (1, 3, 2):
        w_send(k, a, b, a_peer(j))
    w_send(k, a, b, partner)

    p_step(UP_HOPS - lag + 2)
    for j in (1, 3, 2):
        bb = (b + j) % SIDE
        w_wait(k, a, bb)
        for i in (1, 3, 2):
            w_send(k, a, bb, a_peer(i))
        w_send(k, a, bb, partner)
    p_step(UP_HOPS)

    rows = NZ * SLOTS
    for lo in range(0, NZ, 4):
        pr = pall[lo : lo + 4].reshape(4 * SLOTS, width)
        xz = mm(pr, win_ref[...])
        xr = xz.astype(BF)
        sq = xr.astype(F32)
        sq = sq * sq
        sq = sq[:, 0:128] + sq[:, 128:256]
        share = jnp.sum(jnp.transpose(sq), axis=0, keepdims=True)
        st[z, :, lo * SLOTS : (lo + 4) * SLOTS] = jnp.broadcast_to(share, (8, 4 * SLOTS))
        ob[lo * SLOTS : (lo + 4) * SLOTS, :] = mm(xr, wout_ref[...])
    st_step(0)

    heads = width // HD
    kpad[...] = jnp.zeros_like(kpad)
    kpad[0 : keys_ref.shape[0], :] = keys_ref[...].astype(F32)
    own = lax.broadcasted_iota(jnp.int32, (heads * SLOTS, width), 0) // SLOTS
    own = own == lax.broadcasted_iota(jnp.int32, (heads * SLOTS, width), 1) // HD
    kb = jnp.where(own, jnp.concatenate([kpad[...]] * heads, axis=0), 0.0).astype(BF)
    scores = mm_nt(kb, dec_ref[...]) / math.sqrt(HD)
    allowed = lax.broadcasted_iota(jnp.int32, (SLOTS, dec_ref.shape[0]), 0) <= seg_ref[...]
    for h in range(heads):
        sc = jnp.where(allowed, scores[h * SLOTS : (h + 1) * SLOTS], -1e30)
        ex = jnp.exp(sc - jnp.max(sc, axis=0, keepdims=True))
        wts[h * SLOTS : (h + 1) * SLOTS, :] = ex / jnp.sum(ex, axis=0, keepdims=True)

    for t in range(1, UP_HOPS + 1):
        st_step(t)
    for j in (1, 3, 2):
        aa = (a + j) % SIDE
        for i in (0, 1, 3, 2):
            bb = (b + i) % SIDE
            w_wait(k, aa, bb)
            w_send(k, aa, bb, partner)
    for aa in range(SIDE):
        for bb in range(SIDE):
            w_wait(1 - k, aa, bb)

    stat = st[0, 0:1, :]
    for i in range(1, NZ):
        stat += st[i, 0:1, :]
    inv = lax.rsqrt(stat / (NZ * win_ref.shape[1]) + EPS)
    block = 128
    for lo in range(0, rows, block):
        pr = pall[lo // SLOTS : (lo + block) // SLOTS].reshape(block, width)
        r = jnp.transpose(jnp.broadcast_to(inv[:, lo : lo + block], (128, block)))
        r = jnp.concatenate([r] * (pad // 128), axis=1)
        g = mm(pr, wf[:, 0:pad]) * r
        u = mm(pr, wf[:, pad : 2 * pad]) * r
        hid = (g / (1.0 + jnp.exp(-g)) * u).astype(BF)
        ob[lo : lo + block, :] += mm_nt(hid, wf[:, 2 * pad : 3 * pad])

    cut = SLOTS // 2

    def part_of(dest, h):
        return ob[pl.ds(pl.multiple_of(dest * SLOTS + h * cut, cut), cut), :]

    zp_copies, zm_copies = {}, {}
    for t in range(UP_HOPS + 1):
        for h in (0, 1):
            if t < UP_HOPS:
                val = part_of((z + UP_HOPS - t) % NZ, h)
                if t:
                    zp_copies[t - 1, h].wait_recv()
                    val += rzp[t - 1, h].astype(F32)
                szp[t, h] = val.astype(BF)
                c = remote(szp.at[t, h], rzp.at[t, h], zp_s.at[t, h], zp_r.at[t, h], above)
                c.start()
                zp_copies[t, h] = c
            if t < DOWN_HOPS:
                val = part_of((z + NZ - DOWN_HOPS + t) % NZ, h)
                if t:
                    zm_copies[t - 1, h].wait_recv()
                    val += rzm[t - 1, h].astype(F32)
                szm[t, h] = val.astype(BF)
                c = remote(szm.at[t, h], rzm.at[t, h], zm_s.at[t, h], zm_r.at[t, h], below)
                c.start()
                zm_copies[t, h] = c

    wt = jnp.transpose(wts[...]).astype(BF)
    vals = []
    for h in (0, 1):
        zm_copies[DOWN_HOPS - 1, h].wait_recv()
        zp_copies[UP_HOPS - 1, h].wait_recv()
        val = part_of(z, h) + rzp[UP_HOPS - 1, h].astype(F32) + rzm[DOWN_HOPS - 1, h].astype(F32)
        vals.append(val)
    values = jnp.concatenate(vals, axis=0)
    vb = jnp.where(own, jnp.concatenate([values] * heads, axis=0), 0.0).astype(BF)
    out_ref[...] = (dec_ref[...].astype(F32) + mm(wt, vb)).astype(BF)

    for c in raw_sends + rs_copies + w_copies:
        c.wait_send()
    for i in range(SIDE):
        zi = jnp.where(k == 0, SIDE * y + i, SIDE * i + x)
        up_dist = (z - zi + NZ) % NZ
        down_dist = (zi - z + NZ) % NZ
        for part in (0, 1):

            @pl.when(up_dist < UP_HOPS)
            def _():
                bc_send(i, part, True).wait_send()

            @pl.when(down_dist < DOWN_HOPS)
            def _():
                bc_send(i, part, False).wait_send()

    ring_drain(pall, p_sp, p_sm, p_r)
    ring_drain(st, st_sp, st_sm, st_r)
    for c in (*zp_copies.values(), *zm_copies.values()):
        c.wait_send()


def body(enc_states, dec_states, segments, patch_keys, w_in, w_gate, w_up, w_down, w_out):
    nbytes, width = enc_states.shape
    depth, units = w_gate.shape
    quarter = width // 8
    rows = NZ * SLOTS
    dma = pltpu.SemaphoreType.DMA
    vmem = pltpu.VMEM
    return pl.pallas_call(
        kernel,
        out_shape=jax.ShapeDtypeStruct((nbytes, width), BF),
        in_specs=[pl.BlockSpec(memory_space=pltpu.VMEM)] * 9,
        out_specs=pl.BlockSpec(memory_space=pltpu.VMEM),
        scratch_shapes=[
            vmem((SIDE, 2, depth, units), BF),
            vmem((SIDE, 2, depth, units), BF),
            vmem((SIDE, 2, units, depth), BF),
            vmem((SIDE, 2, quarter, w_in.shape[1]), BF),
            vmem((quarter, 1536), BF),
            vmem((3, quarter, 384), BF),
            vmem((width, 1536), BF),
            vmem((NZ, SLOTS, width), BF),
            vmem((8, 128), F32),
            vmem((NZ, 8, rows), F32),
            vmem((rows, width), F32),
            vmem((UP_HOPS, 2, SLOTS // 2, width), BF),
            vmem((UP_HOPS, 2, SLOTS // 2, width), BF),
            vmem((DOWN_HOPS, 2, SLOTS // 2, width), BF),
            vmem((DOWN_HOPS, 2, SLOTS // 2, width), BF),
            vmem((SLOTS, width), F32),
            vmem((width // HD * SLOTS, nbytes), F32),
            dma((7, 3)), dma((SIDE, 2, 3)), dma((3,)),
            dma((SIDE, 2)), dma((SIDE, 2)), dma((SIDE, 2)),
            dma((3,)), dma((3,)), dma((40,)), dma((2, SIDE, SIDE)),
            dma((NZ,)), dma((NZ,)), dma((NZ,)),
            dma((NZ,)), dma((NZ,)), dma((NZ,)),
            dma((UP_HOPS, 2)), dma((UP_HOPS, 2)), dma((DOWN_HOPS, 2)), dma((DOWN_HOPS, 2)),
        ],
        compiler_params=pltpu.CompilerParams(
            collective_id=0, has_side_effects=True, vmem_limit_bytes=60 * 1024 * 1024
        ),
    )(enc_states, dec_states, segments.reshape(1, nbytes), patch_keys, w_in, w_gate, w_up, w_down, w_out)


def solution(mesh):
    placed = (
        P(("seq", "mp"), None),
        P(("seq", "mp"), None),
        P(("seq", "mp")),
        P(("seq", "mp"), None),
        P(None, "mp"),
        P("seq", "mp"),
        P("seq", "mp"),
        P("mp", "seq"),
        P("mp", None),
    )
    return jax.shard_map(
        body, mesh=mesh, in_specs=placed, out_specs=P(("seq", "mp"), None), check_vma=False
    )
```

time: 384 us -> 132 us (0.34)
  blocking collectives: 165 us -> 0 us
  waiting for transfers between devices: 139 us -> 0 us
  Pallas kernels: 0 us -> 126 us
  starting transfers between devices: 25.7 us -> 0 us
  matrix products: 17.9 us -> 0 us
  between operations: 14.2 us -> 0.01 us
  other arithmetic: 10.5 us -> 0 us
    all_to_all x3 -> x0, blocking collectives: 165 us -> none  [the longest x1 104 us: sum_at_owner(): lax.all_to_all(in_blocks(value, dim, peers), axis, 0, 0, tiled=True)]
    all_to_all x4 -> x0, waiting for transfers between devices: 138 us -> none  [the longest x2 99.3 us: copy_for_each(): lax.all_to_all(jnp.broadcast_to(value[None], (peers, *value.shape)), axis...]
    pallas_call x0 -> x1, Pallas kernels: none -> 126 us  [body(): pl.pallas_call(kernel, out_shape=jax.ShapeDtypeStruct((nbytes, width), BF...]
    all_to_all x4 -> x0, starting transfers between devices: 25.6 us -> none  [the longest x2 13.8 us: copy_for_each(): lax.all_to_all(jnp.broadcast_to(value[None], (peers, *value.shape)), axis...]
    dot_general x10 -> x0, matrix products: 17.9 us -> none  [the longest x1 8.72 us: body(): jnp.dot(hidden, lax.all_gather(w_down, 'seq', axis=1, tiled=True), prefer...]
  transfers between devices with their start and end apart: 6 -> 0, of which waited for: 4 -> 0; matrix products, arithmetic and copies ran while one was open for 5% -> 0% of each run, Pallas kernels for 0% -> 0%
where the time goes in v1:
time: 132 us; the launch traced here: 130 us
  Pallas kernels  126 us (95%)
  local copies, waits for them, and re-layouts  4.3 us (3%)
    pallas_call x1, Pallas kernels, body(): pl.pallas_call(kernel, out_shape=jax.ShapeDtypeStruct((nbytes, width), BF...  126 us
    unnamed x5, local copies, waits for them, and re-layouts  4.3 us

profile of v1, /device:TPU:6, one launch (start us, length us, event | category | flops | bytes accessed | tf_op | source)
XLA Modules:
  0.0 129.9 jit_solution(9239188656014011557)
XLA Ops:
  0.0 0.0 copy-start
  0.0 1.7 %copy.10.wg_ref = bf16[128,448]{1,0:T(8,128)(2,1)} copy(bf16[128,448]{0,1:T(8,128)(2,1)} %param.14) | data formatting | bytes 229376 | tf_op args[5]
  1.7 0.0 copy-done
  1.7 0.8 copy.11.wu_ref
  2.5 125.6 %shard_map.91 = bf16[192,1280]{1,0:T(8,128)(2,1)} custom-call(bf16[192,1280]{1,0:T(8,128)(2,1)} %enc_ref.1, bf16[192,1280]{1,0:T(8,128)(2,1)} %dec_ref.1, s32[1,192]{1,0:T(1,128)} %bitcast.1, bf16[31,1280]{1,0:T(8,128)(2,1)} %keys_ref.1, bf16[1280,256]{1,0:T(8,128)(2,1)} %win_ref.1, bf16[128,448]{1,0:T(8,128)(2,1)} %copy.10.wg_ref, ...), custom_call_target="tpu_custom_call" | custom-call | tf_op jit(solution)/shard_map/pallas_call | solution.py:381
  128.1 1.8 %copy.13 = bf16[192,1280]{1,0:T(8,128)(2,1)} copy(bf16[192,1280]{1,0:T(8,128)(2,1)} %shard_map.91) | data formatting | bytes 983040
Async XLA Ops:
  0.0 1.7 %copy-start = (bf16[128,448]{0,1:T(8,128)(2,1)S(1)}, bf16[128,448]{0,1:T(8,128)(2,1)}, u32[]{:S(2)}) copy-start(bf16[128,448]{0,1:T(8,128)(2,1)} %param.15) | copy-start | bytes 344068

commit v2 on v1

v2 whole, which is shorter than its diff:
```python
import math

import jax
import jax.numpy as jnp
from jax import lax
from jax.experimental import pallas as pl
from jax.experimental.pallas import tpu as pltpu
from jax.sharding import PartitionSpec as P

MESH = pl.DeviceIdType.MESH
HD = 128
SIDE = 4
NZ = 16
SLOTS = 32
CUT = SLOTS // 2
BF = jnp.bfloat16
F32 = jnp.float32
EPS = 1e-05
NT = (((1,), (1,)), ((), ()))
UP_HOPS = 8
DOWN_HOPS = 7
PAD = 512
LANES = (2 * PAD // SIDE, PAD // SIDE)


def mm(a, b):
    return jnp.dot(a, b, preferred_element_type=F32)


def mm_nt(a, b):
    return lax.dot_general(a, b, NT, preferred_element_type=F32)


def kernel(
    enc_hbm, dec_hbm, seg_ref, keys_ref, win_hbm, wg_hbm, wu_hbm, wd_hbm, wout_hbm,
    out_ref,
    enc_ref, dec_ref, win_ref, wout_ref,
    rg, ru, rd, bc, ug, ud, rsg, rsd, wf, pall, st, rc, ob, rzp, szp, rzm, szm, kpad, wts,
    in_s, raw_s, raw_r, loc_s, src_s, bc_r, bc_sp, bc_sm, rs_s, rs_r, w_s, w_r,
    p_r, p_sp, p_sm, st_r, st_s, zp_s, zp_r, zm_s, zm_r,
):
    s = lax.axis_index("seq")
    z = lax.axis_index("mp")
    k = s % 2
    x = (s // 2) % SIDE
    y = s // (2 * SIDE)
    a = x + k * (y - x)
    b = y + k * (x - y)
    width = enc_ref.shape[1]
    half = width // 2
    quarter = half // SIDE
    eighth = quarter // 2
    units = wg_hbm.shape[0]

    def dev(xx, yy, kk, zz):
        return {"seq": (yy * SIDE + xx) * 2 + kk, "mp": zz}

    def x_peer(j, kk):
        return dev((x + j) % SIDE, y, kk, z)

    def y_peer(j, kk):
        return dev(x, (y + j) % SIDE, kk, z)

    def a_peer(j):
        return dev((x + j * (1 - k)) % SIDE, (y + j * k) % SIDE, k, z)

    def b_peer(j):
        return dev((x + j * k) % SIDE, (y + j * (1 - k)) % SIDE, k, z)

    def z_peer(j):
        return dev(x, y, k, (z + j) % NZ)

    partner = dev(x, y, 1 - k, z)
    above = z_peer(1)
    below = z_peer(NZ - 1)

    barrier = pltpu.get_barrier_semaphore()
    greeted = [above, below, partner]
    for j in (2, 1, 3):
        for kk in (0, 1):
            greeted += [x_peer(j, kk), y_peer(j, kk)]
    for d in greeted:
        pl.semaphore_signal(barrier, inc=1, device_id=d, device_id_type=MESH)

    def remote(src, dst, ssem, rsem, d):
        return pltpu.make_async_remote_copy(
            src_ref=src, dst_ref=dst, send_sem=ssem, recv_sem=rsem, device_id=d, device_id_type=MESH
        )

    loads = []
    for i, (src, dst) in enumerate(
        ((wout_hbm, wout_ref), (enc_hbm, enc_ref), (win_hbm, win_ref), (dec_hbm, dec_ref))
    ):
        c = pltpu.make_async_copy(src, dst, in_s.at[i])
        c.start()
        loads.append(c)

    def source(zz):
        hit0 = (zz // SIDE) == y
        hit1 = (zz % SIDE) == x
        hit = jnp.where(k == 0, hit0, hit1)
        slot = jnp.where(k == 0, zz % SIDE, zz // SIDE)
        return hit, slot

    first_row = k * half + a * quarter
    hit_me, slot_me = source(z)

    def src_copy(h):
        row = pl.multiple_of(first_row + h * eighth, 16)
        return pltpu.make_async_copy(win_hbm.at[pl.ds(row, eighth), :], bc.at[slot_me, h], src_s.at[h])

    @pl.when(hit_me)
    def _():
        src_copy(0).start()
        src_copy(1).start()

    raws = ((wg_hbm, rg), (wu_hbm, ru), (wd_hbm, rd))
    raw_local = []
    for i, (src, dst) in enumerate(raws):
        c = pltpu.make_async_copy(src, dst.at[a, k], loc_s.at[i])
        c.start()
        raw_local.append(c)

    pl.semaphore_wait(barrier, len(greeted))

    def bc_send(slot, part, up):
        sems = bc_sp if up else bc_sm
        return remote(
            bc.at[slot, part], bc.at[slot, part], sems.at[slot, part], bc_r.at[slot, part],
            above if up else below,
        )

    @pl.when(hit_me)
    def _():
        for h in (0, 1):
            src_copy(h).wait()
            bc_send(slot_me, h, True).start()
            bc_send(slot_me, h, False).start()

    raw_targets = [(partner, b)]
    for j in (1, 3, 2):
        raw_targets += [(x_peer(j, 0), x), (y_peer(j, 1), y)]
    raw_sends = []
    for i, (src, dst) in enumerate(raws):
        for n, (d, slot) in enumerate(raw_targets):
            c = remote(src, dst.at[slot, k], raw_s.at[n, i], raw_r.at[slot, k, i], d)
            c.start()
            raw_sends.append(c)

    loads[0].wait()

    @pl.when(hit_me)
    def _():
        rows = lax.broadcasted_iota(jnp.int32, (quarter, width), 0) + first_row
        cols = lax.broadcasted_iota(jnp.int32, (quarter, width), 1)
        pick = jnp.where(rows == cols, 1.0, 0.0).astype(BF)
        turned = mm_nt(pick, wout_ref[...]).astype(BF)
        for h in (0, 1):
            bc[slot_me, 2 + h] = turned[h * eighth : (h + 1) * eighth]
            bc_send(slot_me, 2 + h, True).start()
            bc_send(slot_me, 2 + h, False).start()

    def bc_step(t, parts):
        if not 1 <= t <= UP_HOPS:
            return
        hit_u, slot_u = source((z + NZ - t) % NZ)
        hit_d, slot_d = source((z + t) % NZ)
        for part in parts:

            @pl.when(hit_u)
            def _():
                bc_send(slot_u, part, True).wait_recv()
                if t < UP_HOPS:
                    bc_send(slot_u, part, True).start()

            if t <= DOWN_HOPS:

                @pl.when(hit_d)
                def _():
                    bc_send(slot_d, part, False).wait_recv()
                    if t < DOWN_HOPS:
                        bc_send(slot_d, part, False).start()

    loads[1].wait()
    member = lax.broadcasted_iota(jnp.int32, (SLOTS, enc_ref.shape[0]), 0) == seg_ref[...]
    member = jnp.where(member, 1.0, 0.0)
    lengths = jnp.maximum(jnp.sum(member, axis=1, keepdims=True), 1.0)
    pall[z] = (mm(member.astype(BF), enc_ref[...]) / lengths).astype(BF)

    def p_send(slot, h, up):
        view = pall.at[slot, pl.ds(h * CUT, CUT), :]
        ssem = p_sp if up else p_sm
        return remote(view, view, ssem.at[slot, h], p_r.at[slot, h], above if up else below)

    def p_step(t):
        if not 0 <= t <= UP_HOPS:
            return
        up_slot = (z + NZ - t) % NZ
        down_slot = (z + t) % NZ
        for h in (0, 1):
            if t:
                p_send(up_slot, h, True).wait_recv()
            if t < UP_HOPS:
                p_send(up_slot, h, True).start()
            if 1 <= t <= DOWN_HOPS:
                p_send(down_slot, h, False).wait_recv()
            if t < DOWN_HOPS:
                p_send(down_slot, h, False).start()

    ug[...] = jnp.zeros_like(ug)
    ud[...] = jnp.zeros_like(ud)
    lag = 2
    for t in range(1, UP_HOPS + 1):
        bc_step(t, (0, 1))
        bc_step(t - 1, (2, 3))
        p_step(t - lag)

    def raw_wait(i):
        raw_local[i].wait()
        src, dst = raws[i]
        for d in range(SIDE):
            for kk in (0, 1):

                @pl.when(jnp.logical_or(a != d, k != kk))
                def _():
                    remote(src, dst.at[d, kk], raw_s.at[0, 0], raw_r.at[d, kk, i], partner).wait_recv()

    def deep(buf):
        return jnp.concatenate([buf[i, kk] for i in range(SIDE) for kk in (0, 1)], axis=1)

    def tall(part):
        return jnp.concatenate(
            [jnp.concatenate([bc[i, part + h] for i in range(SIDE)], axis=1) for h in (0, 1)], axis=0
        )

    rs_copies = [[], []]

    def piece(part, bb, base=0):
        return pl.ds(pl.multiple_of(base + bb * LANES[part], 128), LANES[part])

    def rs_send(part):
        src, dst = ((ug, rsg), (ud, rsd))[part]
        for j in (2, 1, 3):
            c = remote(
                src.at[:, piece(part, (b + j) % SIDE)], dst.at[j - 1],
                rs_s.at[part, j - 1], rs_r.at[part, j - 1], b_peer(j),
            )
            c.start()
            rs_copies[part].append(c)

    raw_wait(0)
    raw_wait(1)
    ins = tall(0)
    ug[:, 0:units] = mm_nt(ins, deep(rg)).astype(BF)
    ug[:, PAD : PAD + units] = mm_nt(ins, deep(ru)).astype(BF)
    rs_send(0)
    bc_step(UP_HOPS, (2, 3))
    p_step(UP_HOPS - lag + 1)
    raw_wait(2)
    outs = tall(2)
    down = jnp.zeros((quarter, units), F32)
    for i in range(SIDE):
        for kk in (0, 1):
            down += mm_nt(
                outs[:, (2 * i + kk) * HD : (2 * i + kk + 1) * HD], rd[i, kk]
            )
    ud[:, 0:units] = down.astype(BF)
    rs_send(1)

    def place(part, kk, aa, bb):
        row = pl.multiple_of(kk * half + aa * quarter, 32)
        return wf.at[pl.ds(row, quarter), piece(part, bb, part * 2 * PAD)]

    w_copies = []

    def w_send(part, kk, aa, bb, d):
        n = len(w_copies)
        view = place(part, kk, aa, bb)
        c = remote(view, view, w_s.at[n], w_r.at[part, kk, aa, bb], d)
        c.start()
        w_copies.append(c)

    def w_wait(part, kk, aa, bb):
        view = place(part, kk, aa, bb)
        remote(view, view, w_s.at[0], w_r.at[part, kk, aa, bb], partner).wait_recv()

    def w_sum(part):
        src, got = ((ug, rsg), (ud, rsd))[part]
        total = src[:, piece(part, b)].astype(F32)
        for c in rs_copies[part]:
            c.wait_recv()
        for j in (0, 1, 2):
            total += got[j].astype(F32)
        place(part, k, a, b)[...] = total.astype(BF)
        for j in (2, 1, 3):
            w_send(part, k, a, b, b_peer(j))
        for j in (2, 1, 3):
            w_send(part, k, a, b, a_peer(j))
        w_send(part, k, a, b, partner)

    def w_pass(part):
        for j in (1, 3, 2):
            bb = (b + j) % SIDE
            w_wait(part, k, a, bb)
            for i in (2, 1, 3):
                w_send(part, k, a, bb, a_peer(i))
            w_send(part, k, a, bb, partner)

    w_sum(0)
    p_step(UP_HOPS - lag + 2)
    w_sum(1)
    w_pass(0)

    loads[2].wait()
    rows = NZ * SLOTS
    for lo in range(0, NZ, 4):
        pr = pall[lo : lo + 4].reshape(4 * SLOTS, width)
        xr = mm(pr, win_ref[...]).astype(BF)
        sq = xr.astype(F32)
        sq = sq * sq
        sq = sq[:, 0:128] + sq[:, 128:256]
        st[z, :, lo * SLOTS : (lo + 4) * SLOTS] = jnp.sum(jnp.transpose(sq), axis=0, keepdims=True)
        ob[lo * SLOTS : (lo + 4) * SLOTS, :] = mm(xr, wout_ref[...])
    st_copies = []
    for j in (8, 7, 9, 6, 10, 5, 11, 4, 12, 3, 13, 2, 14, 1, 15):
        c = remote(st.at[z], st.at[z], st_s.at[j], st_r.at[z], z_peer(j))
        c.start()
        st_copies.append(c)
    w_pass(1)

    loads[3].wait()
    heads = width // HD
    kpad[...] = jnp.zeros_like(kpad)
    kpad[0 : keys_ref.shape[0], :] = keys_ref[...].astype(F32)
    own = lax.broadcasted_iota(jnp.int32, (heads * SLOTS, width), 0) // SLOTS
    own = own == lax.broadcasted_iota(jnp.int32, (heads * SLOTS, width), 1) // HD
    kb = jnp.where(own, jnp.concatenate([kpad[...]] * heads, axis=0), 0.0).astype(BF)
    scores = mm_nt(kb, dec_ref[...]) / math.sqrt(HD)
    allowed = lax.broadcasted_iota(jnp.int32, (SLOTS, dec_ref.shape[0]), 0) <= seg_ref[...]
    for h in range(heads):
        sc = jnp.where(allowed, scores[h * SLOTS : (h + 1) * SLOTS], -1e30)
        ex = jnp.exp(sc - jnp.max(sc, axis=0, keepdims=True))
        wts[h * SLOTS : (h + 1) * SLOTS, :] = ex / jnp.sum(ex, axis=0, keepdims=True)
    wt = jnp.transpose(wts[...]).astype(BF)

    for part in (0, 1):
        for j in (1, 3, 2):
            aa = (a + j) % SIDE
            for i in (0, 1, 3, 2):
                bb = (b + i) % SIDE
                w_wait(part, k, aa, bb)
                w_send(part, k, aa, bb, partner)

    for j in range(1, NZ):
        slot = (z + j) % NZ
        remote(st.at[slot], st.at[slot], st_s.at[0], st_r.at[slot], above).wait_recv()
    stat = st[0]
    for i in range(1, NZ):
        stat += st[i]
    inv = lax.rsqrt(stat / (NZ * win_ref.shape[1]) + EPS)
    for i in range(0, NZ, 4):
        r = jnp.transpose(jnp.broadcast_to(inv[:, i * SLOTS : (i + 4) * SLOTS], (HD, 4 * SLOTS)))
        rc[i : i + 4] = r.reshape(4, SLOTS, HD)

    for part in (0, 1):
        for aa in range(SIDE):
            for bb in range(SIDE):
                w_wait(part, 1 - k, aa, bb)

    def ffn(t):
        d1 = (z + UP_HOPS - t) % NZ
        d2 = (z + NZ - DOWN_HOPS + t) % NZ
        pr = jnp.concatenate([pall[d1], pall[d2]], axis=0)
        r = jnp.concatenate([rc[d1], rc[d2]], axis=0)
        r = jnp.concatenate([r] * (PAD // HD), axis=1)
        g = mm(pr, wf[:, 0:PAD]) * r
        u = mm(pr, wf[:, PAD : 2 * PAD]) * r
        hid = (g / (1.0 + jnp.exp(-g)) * u).astype(BF)
        o = mm_nt(hid, wf[:, 2 * PAD : 3 * PAD])
        row1 = pl.multiple_of(d1 * SLOTS, SLOTS)
        row2 = pl.multiple_of(d2 * SLOTS, SLOTS)
        return (
            o[0:SLOTS] + ob[pl.ds(row1, SLOTS), :],
            o[SLOTS : 2 * SLOTS] + ob[pl.ds(row2, SLOTS), :],
        )

    zp_copies, zm_copies = {}, {}
    for t in range(UP_HOPS):
        up_val, down_val = ffn(t)
        for h in (0, 1):
            val = up_val[h * CUT : (h + 1) * CUT]
            if t:
                zp_copies[t - 1, h].wait_recv()
                val += rzp[t - 1, h].astype(F32)
            szp[t, h] = val.astype(BF)
            c = remote(szp.at[t, h], rzp.at[t, h], zp_s.at[t, h], zp_r.at[t, h], above)
            c.start()
            zp_copies[t, h] = c
            if t < DOWN_HOPS:
                val = down_val[h * CUT : (h + 1) * CUT]
                if t:
                    zm_copies[t - 1, h].wait_recv()
                    val += rzm[t - 1, h].astype(F32)
                szm[t, h] = val.astype(BF)
                c = remote(szm.at[t, h], rzm.at[t, h], zm_s.at[t, h], zm_r.at[t, h], below)
                c.start()
                zm_copies[t, h] = c

    vals = []
    for h in (0, 1):
        zm_copies[DOWN_HOPS - 1, h].wait_recv()
        val = down_val[h * CUT : (h + 1) * CUT] + rzm[DOWN_HOPS - 1, h].astype(F32)
        zp_copies[UP_HOPS - 1, h].wait_recv()
        vals.append(val + rzp[UP_HOPS - 1, h].astype(F32))
    values = jnp.concatenate(vals, axis=0)
    vb = jnp.where(own, jnp.concatenate([values] * heads, axis=0), 0.0).astype(BF)
    out_ref[...] = mm(wt, vb)

    for c in raw_sends + rs_copies[0] + rs_copies[1] + w_copies + st_copies:
        c.wait_send()
    for i in range(SIDE):
        zi = jnp.where(k == 0, SIDE * y + i, SIDE * i + x)
        up_dist = (z - zi + NZ) % NZ
        down_dist = (zi - z + NZ) % NZ
        for part in range(4):

            @pl.when(up_dist < UP_HOPS)
            def _():
                bc_send(i, part, True).wait_send()

            @pl.when(down_dist < DOWN_HOPS)
            def _():
                bc_send(i, part, False).wait_send()

    for h in (0, 1):
        for t in range(UP_HOPS):
            p_send((z + NZ - t) % NZ, h, True).wait_send()
        for t in range(DOWN_HOPS):
            p_send((z + t) % NZ, h, False).wait_send()
    for c in (*zp_copies.values(), *zm_copies.values()):
        c.wait_send()


def body(enc_states, dec_states, segments, patch_keys, w_in, w_gate, w_up, w_down, w_out):
    nbytes, width = enc_states.shape
    depth, units = w_gate.shape
    local = w_in.shape[1]
    quarter = width // 8
    rows = NZ * SLOTS
    dma = pltpu.SemaphoreType.DMA
    vmem = pltpu.VMEM
    hbm = pl.BlockSpec(memory_space=pl.ANY)
    here = pl.BlockSpec(memory_space=pltpu.VMEM)
    mixed = pl.pallas_call(
        kernel,
        out_shape=jax.ShapeDtypeStruct((nbytes, width), F32),
        in_specs=[hbm, hbm, here, here, hbm, hbm, hbm, hbm, hbm],
        out_specs=here,
        scratch_shapes=[
            vmem((nbytes, width), BF),
            vmem((nbytes, width), BF),
            vmem((width, local), BF),
            vmem((local, width), BF),
            vmem((SIDE, 2, units, depth), BF),
            vmem((SIDE, 2, units, depth), BF),
            vmem((SIDE, 2, units, depth), BF),
            vmem((SIDE, 4, quarter // 2, local), BF),
            vmem((quarter, 2 * PAD), BF),
            vmem((quarter, PAD), BF),
            vmem((3, quarter, LANES[0]), BF),
            vmem((3, quarter, LANES[1]), BF),
            vmem((width, 3 * PAD), BF),
            vmem((NZ, SLOTS, width), BF),
            vmem((NZ, 1, rows), F32),
            vmem((NZ, SLOTS, HD), F32),
            vmem((rows, width), F32),
            vmem((UP_HOPS, 2, CUT, width), BF),
            vmem((UP_HOPS, 2, CUT, width), BF),
            vmem((DOWN_HOPS, 2, CUT, width), BF),
            vmem((DOWN_HOPS, 2, CUT, width), BF),
            vmem((SLOTS, width), F32),
            vmem((width // HD * SLOTS, nbytes), F32),
            dma((4,)), dma((7, 3)), dma((SIDE, 2, 3)), dma((3,)), dma((2,)),
            dma((SIDE, 4)), dma((SIDE, 4)), dma((SIDE, 4)),
            dma((2, 3)), dma((2, 3)), dma((62,)), dma((2, 2, SIDE, SIDE)),
            dma((NZ, 2)), dma((NZ, 2)), dma((NZ, 2)),
            dma((NZ,)), dma((NZ,)),
            dma((UP_HOPS, 2)), dma((UP_HOPS, 2)), dma((DOWN_HOPS, 2)), dma((DOWN_HOPS, 2)),
        ],
        compiler_params=pltpu.CompilerParams(
            collective_id=0, has_side_effects=True, vmem_limit_bytes=60 * 1024 * 1024
        ),
    )(
        enc_states, dec_states, segments.reshape(1, nbytes), patch_keys, w_in,
        w_gate.T, w_up.T, w_down, w_out,
    )
    return (dec_states.astype(F32) + mixed).astype(BF)


def solution(mesh):
    placed = (
        P(("seq", "mp"), None),
        P(("seq", "mp"), None),
        P(("seq", "mp")),
        P(("seq", "mp"), None),
        P(None, "mp"),
        P("seq", "mp"),
        P("seq", "mp"),
        P("mp", "seq"),
        P("mp", None),
    )
    return jax.shard_map(
        body, mesh=mesh, in_specs=placed, out_specs=P(("seq", "mp"), None), check_vma=False
    )
```

time: 132 us -> 107 us (0.81); the launches traced: 130 us -> 107 us
  Pallas kernels: 126 us -> 105 us
  local copies, waits for them, and re-layouts: 4.3 us -> 0.01 us
  other arithmetic: 0 us -> 2.06 us
    pallas_call x1, Pallas kernels: 126 us -> 105 us  [body(): pl.pallas_call(kernel, out_shape=jax.ShapeDtypeStruct((nbytes, width), F3...]
    unnamed x5 -> x2, local copies, waits for them, and re-layouts: 4.3 us -> 0.01 us
    convert_element_type x0 -> x1, other arithmetic: none -> 2.06 us  [body(): return (dec_states.astype(F32) + mixed).astype(BF)]
where the time goes in v2:
time: 107 us
  Pallas kernels  105 us (98%)
  other arithmetic  2.06 us (2%)
    pallas_call x1, Pallas kernels, body(): pl.pallas_call(kernel, out_shape=jax.ShapeDtypeStruct((nbytes, width), F3...  105 us

profile of v2, /device:TPU:6, one launch (start us, length us, event | category | flops | bytes accessed | tf_op | source)
XLA Modules:
  0.0 106.8 jit_solution(5258725328413231588)
XLA Ops:
  0.0 0.0 copy-start
  0.0 104.7 %shard_map.91 = f32[192,1280]{1,0:T(8,128)} custom-call(bf16[192,1280]{1,0:T(8,128)(2,1)} %enc_hbm.1, bf16[192,1280]{1,0:T(8,128)(2,1)} %dec_hbm.1, s32[1,192]{1,0:T(1,128)} %bitcast.5, bf16[31,1280]{1,0:T(8,128)(2,1)} %keys_ref.1, bf16[1280,256]{1,0:T(8,128)(2,1)} %win_hbm.1, bf16[448,128]{1,0:T(8,128)(2,1)} %bitcast.3, bf16[448,128]{1,0:T(8,128)(2,1)} %bitcast.4, ...), custom_call_target="tpu_custom_call" | custom-call | tf_op jit(solution)/shard_map/pallas_call | solution.py:454
  104.7 0.0 copy-done
  104.7 2.1 %add_convert_fusion = bf16[192,1280]{1,0:T(8,128)(2,1)} fusion(f32[192,1280]{1,0:T(8,128)} %shard_map.91, bf16[192,1280]{1,0:T(8,128)(2,1)S(1)} %copy-done), kind=kLoop, calls=%fused_computation | loop fusion | flops 737280 | bytes 1966080 | tf_op jit(solution)/shard_map/convert_element_type | solution.py:497
Async XLA Ops:
  0.0 104.7 %copy-start = (bf16[192,1280]{1,0:T(8,128)(2,1)S(1)}, bf16[192,1280]{1,0:T(8,128)(2,1)}, u32[]{:S(2)}) copy-start(bf16[192,1280]{1,0:T(8,128)(2,1)} %dec_hbm.1) | copy-start | bytes 1474564

commit v3 on v2

--- a/solution.py
+++ b/solution.py
@@ -13,6 +13,7 @@
 NZ = 16
 SLOTS = 32
 CUT = SLOTS // 2
+CHUNKS = 4
 BF = jnp.bfloat16
 F32 = jnp.float32
 EPS = 1e-05
@@ -35,8 +36,8 @@
     enc_hbm, dec_hbm, seg_ref, keys_ref, win_hbm, wg_hbm, wu_hbm, wd_hbm, wout_hbm,
     out_ref,
     enc_ref, dec_ref, win_ref, wout_ref,
-    rg, ru, rd, bc, ug, ud, rsg, rsd, wf, pall, st, rc, ob, rzp, szp, rzm, szm, kpad, wts,
-    in_s, raw_s, raw_r, loc_s, src_s, bc_r, bc_sp, bc_sm, rs_s, rs_r, w_s, w_r,
+    rg, ru, rd, bc, ug, ud, rsg, rsd, wf, pall, st, rc, xs, ob, rzp, szp, rzm, szm, kpad, wts,
+    in_s, raw_s, raw_r, loc_s, src_s, bc_r, bc_sp, bc_sm, rs_s, rs_r, w_s, w_r, h_r,
     p_r, p_sp, p_sm, st_r, st_s, zp_s, zp_r, zm_s, zm_r,
 ):
     s = lax.axis_index("seq")
@@ -188,7 +189,7 @@
     pall[z] = (mm(member.astype(BF), enc_ref[...]) / lengths).astype(BF)
 
     def p_send(slot, h, up):
-        view = pall.at[slot, pl.ds(h * CUT, CUT), :]
+        view = pall.at[slot, pl.ds(h // 2 * CUT, CUT), pl.ds(h % 2 * half, half)]
         ssem = p_sp if up else p_sm
         return remote(view, view, ssem.at[slot, h], p_r.at[slot, h], above if up else below)
 
@@ -197,7 +198,7 @@
             return
         up_slot = (z + NZ - t) % NZ
         down_slot = (z + t) % NZ
-        for h in (0, 1):
+        for h in range(CHUNKS):
             if t:
                 p_send(up_slot, h, True).wait_recv()
             if t < UP_HOPS:
@@ -209,7 +210,7 @@
 
     ug[...] = jnp.zeros_like(ug)
     ud[...] = jnp.zeros_like(ud)
-    lag = 2
+    lag = 4
     for t in range(1, UP_HOPS + 1):
         bc_step(t, (0, 1))
         bc_step(t - 1, (2, 3))
@@ -257,15 +258,9 @@
     bc_step(UP_HOPS, (2, 3))
     p_step(UP_HOPS - lag + 1)
     raw_wait(2)
-    outs = tall(2)
-    down = jnp.zeros((quarter, units), F32)
-    for i in range(SIDE):
-        for kk in (0, 1):
-            down += mm_nt(
-                outs[:, (2 * i + kk) * HD : (2 * i + kk + 1) * HD], rd[i, kk]
-            )
-    ud[:, 0:units] = down.astype(BF)
+    ud[:, 0:units] = mm_nt(tall(2), deep(rd)).astype(BF)
     rs_send(1)
+    p_step(UP_HOPS - lag + 2)
 
     def place(part, kk, aa, bb):
         row = pl.multiple_of(kk * half + aa * quarter, 32)
@@ -277,6 +272,17 @@
         n = len(w_copies)
         view = place(part, kk, aa, bb)
         c = remote(view, view, w_s.at[n], w_r.at[part, kk, aa, bb], d)
+        c.start()
+        w_copies.append(c)
+
+    def w_half(part, aa, bb, h):
+        row = pl.multiple_of(k * half + aa * quarter + h * eighth, 16)
+        return wf.at[pl.ds(row, eighth), piece(part, bb, part * 2 * PAD)]
+
+    def w_relay(part, aa, bb, h, d):
+        n = len(w_copies)
+        view = w_half(part, aa, bb, h)
+        c = remote(view, view, w_s.at[n], h_r.at[part, bb, h], d)
         c.start()
         w_copies.append(c)
 
@@ -294,7 +300,7 @@
         place(part, k, a, b)[...] = total.astype(BF)
         for j in (2, 1, 3):
             w_send(part, k, a, b, b_peer(j))
-        for j in (2, 1, 3):
+        for j in (1, 3):
             w_send(part, k, a, b, a_peer(j))
         w_send(part, k, a, b, partner)
 
@@ -302,13 +308,14 @@
         for j in (1, 3, 2):
             bb = (b + j) % SIDE
             w_wait(part, k, a, bb)
-            for i in (2, 1, 3):
+            for i in (1, 3):
                 w_send(part, k, a, bb, a_peer(i))
             w_send(part, k, a, bb, partner)
 
     w_sum(0)
-    p_step(UP_HOPS - lag + 2)
+    p_step(UP_HOPS - lag + 3)
     w_sum(1)
+    p_step(UP_HOPS - lag + 4)
     w_pass(0)
 
     loads[2].wait()
@@ -316,17 +323,19 @@
     for lo in range(0, NZ, 4):
         pr = pall[lo : lo + 4].reshape(4 * SLOTS, width)
         xr = mm(pr, win_ref[...]).astype(BF)
+        xs[lo * SLOTS : (lo + 4) * SLOTS, :] = xr
         sq = xr.astype(F32)
         sq = sq * sq
         sq = sq[:, 0:128] + sq[:, 128:256]
         st[z, :, lo * SLOTS : (lo + 4) * SLOTS] = jnp.sum(jnp.transpose(sq), axis=0, keepdims=True)
-        ob[lo * SLOTS : (lo + 4) * SLOTS, :] = mm(xr, wout_ref[...])
     st_copies = []
     for j in (8, 7, 9, 6, 10, 5, 11, 4, 12, 3, 13, 2, 14, 1, 15):
         c = remote(st.at[z], st.at[z], st_s.at[j], st_r.at[z], z_peer(j))
         c.start()
         st_copies.append(c)
     w_pass(1)
+    for lo in range(0, rows, 4 * SLOTS):
+        ob[lo : lo + 4 * SLOTS, :] = mm(xs[lo : lo + 4 * SLOTS, :], wout_ref[...])
 
     loads[3].wait()
     heads = width // HD
@@ -344,12 +353,20 @@
     wt = jnp.transpose(wts[...]).astype(BF)
 
     for part in (0, 1):
-        for j in (1, 3, 2):
-            aa = (a + j) % SIDE
-            for i in (0, 1, 3, 2):
-                bb = (b + i) % SIDE
+        for i in (0, 1, 3, 2):
+            bb = (b + i) % SIDE
+            for j in (1, 3):
+                aa = (a + j) % SIDE
                 w_wait(part, k, aa, bb)
+                w_relay(part, aa, bb, j // 2, a_peer(SIDE - j))
                 w_send(part, k, aa, bb, partner)
+        for i in (0, 1, 3, 2):
+            bb = (b + i) % SIDE
+            aa = (a + 2) % SIDE
+            for h in (0, 1):
+                view = w_half(part, aa, bb, h)
+                remote(view, view, w_s.at[0], h_r.at[part, bb, h], partner).wait_recv()
+            w_send(part, k, aa, bb, partner)
 
     for j in range(1, NZ):
         slot = (z + j) % NZ
@@ -384,11 +401,14 @@
             o[SLOTS : 2 * SLOTS] + ob[pl.ds(row2, SLOTS), :],
         )
 
+    def chunk(val, h):
+        return val[h // 2 * CUT : (h // 2 + 1) * CUT, h % 2 * half : (h % 2 + 1) * half]
+
     zp_copies, zm_copies = {}, {}
     for t in range(UP_HOPS):
         up_val, down_val = ffn(t)
-        for h in (0, 1):
-            val = up_val[h * CUT : (h + 1) * CUT]
+        for h in range(CHUNKS):
+            val = chunk(up_val, h)
             if t:
                 zp_copies[t - 1, h].wait_recv()
                 val += rzp[t - 1, h].astype(F32)
@@ -397,7 +417,7 @@
             c.start()
             zp_copies[t, h] = c
             if t < DOWN_HOPS:
-                val = down_val[h * CUT : (h + 1) * CUT]
+                val = chunk(down_val, h)
                 if t:
                     zm_copies[t - 1, h].wait_recv()
                     val += rzm[t - 1, h].astype(F32)
@@ -407,12 +427,14 @@
                 zm_copies[t, h] = c
 
     vals = []
-    for h in (0, 1):
+    for h in range(CHUNKS):
         zm_copies[DOWN_HOPS - 1, h].wait_recv()
-        val = down_val[h * CUT : (h + 1) * CUT] + rzm[DOWN_HOPS - 1, h].astype(F32)
+        val = chunk(down_val, h) + rzm[DOWN_HOPS - 1, h].astype(F32)
         zp_copies[UP_HOPS - 1, h].wait_recv()
         vals.append(val + rzp[UP_HOPS - 1, h].astype(F32))
-    values = jnp.concatenate(vals, axis=0)
+    values = jnp.concatenate(
+        [jnp.concatenate(vals[i : i + 2], axis=1) for i in (0, 2)], axis=0
+    )
     vb = jnp.where(own, jnp.concatenate([values] * heads, axis=0), 0.0).astype(BF)
     out_ref[...] = mm(wt, vb)
 
@@ -432,7 +454,7 @@
             def _():
                 bc_send(i, part, False).wait_send()
 
-    for h in (0, 1):
+    for h in range(CHUNKS):
         for t in range(UP_HOPS):
             p_send((z + NZ - t) % NZ, h, True).wait_send()
         for t in range(DOWN_HOPS):
@@ -473,19 +495,20 @@
             vmem((NZ, SLOTS, width), BF),
             vmem((NZ, 1, rows), F32),
             vmem((NZ, SLOTS, HD), F32),
+            vmem((rows, local), BF),
             vmem((rows, width), F32),
-            vmem((UP_HOPS, 2, CUT, width), BF),
-            vmem((UP_HOPS, 2, CUT, width), BF),
-            vmem((DOWN_HOPS, 2, CUT, width), BF),
-            vmem((DOWN_HOPS, 2, CUT, width), BF),
+            vmem((UP_HOPS, CHUNKS, CUT, width // 2), BF),
+            vmem((UP_HOPS, CHUNKS, CUT, width // 2), BF),
+            vmem((DOWN_HOPS, CHUNKS, CUT, width // 2), BF),
+            vmem((DOWN_HOPS, CHUNKS, CUT, width // 2), BF),
             vmem((SLOTS, width), F32),
             vmem((width // HD * SLOTS, nbytes), F32),
             dma((4,)), dma((7, 3)), dma((SIDE, 2, 3)), dma((3,)), dma((2,)),
             dma((SIDE, 4)), dma((SIDE, 4)), dma((SIDE, 4)),
-            dma((2, 3)), dma((2, 3)), dma((62,)), dma((2, 2, SIDE, SIDE)),
-            dma((NZ, 2)), dma((NZ, 2)), dma((NZ, 2)),
+            dma((2, 3)), dma((2, 3)), dma((72,)), dma((2, 2, SIDE, SIDE)), dma((2, SIDE, 2)),
+            dma((NZ, CHUNKS)), dma((NZ, CHUNKS)), dma((NZ, CHUNKS)),
             dma((NZ,)), dma((NZ,)),
-            dma((UP_HOPS, 2)), dma((UP_HOPS, 2)), dma((DOWN_HOPS, 2)), dma((DOWN_HOPS, 2)),
+            dma((UP_HOPS, CHUNKS)), dma((UP_HOPS, CHUNKS)), dma((DOWN_HOPS, CHUNKS)), dma((DOWN_HOPS, CHUNKS)),
         ],
         compiler_params=pltpu.CompilerParams(
             collective_id=0, has_side_effects=True, vmem_limit_bytes=60 * 1024 * 1024

time: 107 us -> 109 us (1.019); the launches traced: 107 us -> 107 us
  no operation moved by 1% of the time
where the time goes in v3:
time: 109 us; the launch traced here: 107 us
  Pallas kernels  105 us (96%)
  other arithmetic  2.06 us (2%)
    pallas_call x1, Pallas kernels, body(): pl.pallas_call(kernel, out_shape=jax.ShapeDtypeStruct((nbytes, width), F3...  105 us

profile of v3, /device:TPU:6, one launch (start us, length us, event | category | flops | bytes accessed | tf_op | source)
XLA Modules:
  0.0 107.3 jit_solution(2310824278435395403)
XLA Ops:
  0.0 0.0 copy-start
  0.0 105.2 %shard_map.91 = f32[192,1280]{1,0:T(8,128)} custom-call(bf16[192,1280]{1,0:T(8,128)(2,1)} %enc_hbm.1, bf16[192,1280]{1,0:T(8,128)(2,1)} %dec_hbm.1, s32[1,192]{1,0:T(1,128)} %bitcast.5, bf16[31,1280]{1,0:T(8,128)(2,1)} %keys_ref.1, bf16[1280,256]{1,0:T(8,128)(2,1)} %win_hbm.1, bf16[448,128]{1,0:T(8,128)(2,1)} %bitcast.3, bf16[448,128]{1,0:T(8,128)(2,1)} %bitcast.4, ...), custom_call_target="tpu_custom_call" | custom-call | tf_op jit(solution)/shard_map/pallas_call | solution.py:476
  105.3 0.0 copy-done
  105.3 2.1 %add_convert_fusion = bf16[192,1280]{1,0:T(8,128)(2,1)} fusion(f32[192,1280]{1,0:T(8,128)} %shard_map.91, bf16[192,1280]{1,0:T(8,128)(2,1)S(1)} %copy-done), kind=kLoop, calls=%fused_computation | loop fusion | flops 737280 | bytes 1966080 | tf_op jit(solution)/shard_map/convert_element_type | solution.py:520
Async XLA Ops:
  0.0 105.3 %copy-start = (bf16[192,1280]{1,0:T(8,128)(2,1)S(1)}, bf16[192,1280]{1,0:T(8,128)(2,1)}, u32[]{:S(2)}) copy-start(bf16[192,1280]{1,0:T(8,128)(2,1)} %dec_hbm.1) | copy-start | bytes 1474564

commit v4 on v2

--- a/solution.py
+++ b/solution.py
@@ -35,7 +35,7 @@
     enc_hbm, dec_hbm, seg_ref, keys_ref, win_hbm, wg_hbm, wu_hbm, wd_hbm, wout_hbm,
     out_ref,
     enc_ref, dec_ref, win_ref, wout_ref,
-    rg, ru, rd, bc, ug, ud, rsg, rsd, wf, pall, st, rc, ob, rzp, szp, rzm, szm, kpad, wts,
+    rg, ru, rd, bc, ug, ud, rsg, rsd, wf, pall, st, rc, xs, ob, rzp, szp, rzm, szm, kpad, wts,
     in_s, raw_s, raw_r, loc_s, src_s, bc_r, bc_sp, bc_sm, rs_s, rs_r, w_s, w_r,
     p_r, p_sp, p_sm, st_r, st_s, zp_s, zp_r, zm_s, zm_r,
 ):
@@ -75,7 +75,9 @@
     below = z_peer(NZ - 1)
 
     barrier = pltpu.get_barrier_semaphore()
-    greeted = [above, below, partner]
+    above2 = z_peer(2)
+    below2 = z_peer(NZ - 2)
+    greeted = [above2, below2, above, below, partner]
     for j in (2, 1, 3):
         for kk in (0, 1):
             greeted += [x_peer(j, kk), y_peer(j, kk)]
@@ -123,19 +125,23 @@
 
     pl.semaphore_wait(barrier, len(greeted))
 
-    def bc_send(slot, part, up):
+    def bc_send(slot, part, up, far=0):
         sems = bc_sp if up else bc_sm
-        return remote(
-            bc.at[slot, part], bc.at[slot, part], sems.at[slot, part], bc_r.at[slot, part],
-            above if up else below,
-        )
+        target = ((below, below2), (above, above2))[up][far]
+        view = bc.at[slot, part]
+        return remote(view, view, sems.at[slot, part, far], bc_r.at[slot, part], target)
+
+    def bc_spread(slot, part, up, far=True):
+        if far:
+            bc_send(slot, part, up, 1).start()
+        bc_send(slot, part, up, 0).start()
 
     @pl.when(hit_me)
     def _():
         for h in (0, 1):
             src_copy(h).wait()
-            bc_send(slot_me, h, True).start()
-            bc_send(slot_me, h, False).start()
+            bc_spread(slot_me, h, True)
+            bc_spread(slot_me, h, False)
 
     raw_targets = [(partner, b)]
     for j in (1, 3, 2):
@@ -157,29 +163,30 @@
         turned = mm_nt(pick, wout_ref[...]).astype(BF)
         for h in (0, 1):
             bc[slot_me, 2 + h] = turned[h * eighth : (h + 1) * eighth]
-            bc_send(slot_me, 2 + h, True).start()
-            bc_send(slot_me, 2 + h, False).start()
+            bc_spread(slot_me, 2 + h, True)
+            bc_spread(slot_me, 2 + h, False)
 
     def bc_step(t, parts):
-        if not 1 <= t <= UP_HOPS:
+        if not 1 <= t <= UP_HOPS // 2:
             return
-        hit_u, slot_u = source((z + NZ - t) % NZ)
-        hit_d, slot_d = source((z + t) % NZ)
-        for part in parts:
-
-            @pl.when(hit_u)
-            def _():
-                bc_send(slot_u, part, True).wait_recv()
-                if t < UP_HOPS:
-                    bc_send(slot_u, part, True).start()
-
-            if t <= DOWN_HOPS:
-
-                @pl.when(hit_d)
+        for dist in (2 * t, 2 * t - 1):
+            hit_u, slot_u = source((z + NZ - dist) % NZ)
+            hit_d, slot_d = source((z + dist) % NZ)
+            for part in parts:
+
+                @pl.when(hit_u)
                 def _():
-                    bc_send(slot_d, part, False).wait_recv()
-                    if t < DOWN_HOPS:
-                        bc_send(slot_d, part, False).start()
+                    bc_send(slot_u, part, True).wait_recv()
+                    if dist % 2 == 0 and dist < UP_HOPS:
+                        bc_spread(slot_u, part, True)
+
+                if dist <= DOWN_HOPS:
+
+                    @pl.when(hit_d)
+                    def _():
+                        bc_send(slot_d, part, False).wait_recv()
+                        if dist % 2 == 0 and dist < DOWN_HOPS:
+                            bc_spread(slot_d, part, False, dist + 2 <= DOWN_HOPS)
 
     loads[1].wait()
     member = lax.broadcasted_iota(jnp.int32, (SLOTS, enc_ref.shape[0]), 0) == seg_ref[...]
@@ -209,11 +216,11 @@
 
     ug[...] = jnp.zeros_like(ug)
     ud[...] = jnp.zeros_like(ud)
-    lag = 2
-    for t in range(1, UP_HOPS + 1):
+    p_step(0)
+    for t in range(1, 5):
         bc_step(t, (0, 1))
+        p_step(t)
         bc_step(t - 1, (2, 3))
-        p_step(t - lag)
 
     def raw_wait(i):
         raw_local[i].wait()
@@ -254,17 +261,10 @@
     ug[:, 0:units] = mm_nt(ins, deep(rg)).astype(BF)
     ug[:, PAD : PAD + units] = mm_nt(ins, deep(ru)).astype(BF)
     rs_send(0)
-    bc_step(UP_HOPS, (2, 3))
-    p_step(UP_HOPS - lag + 1)
+    bc_step(4, (2, 3))
+    p_step(5)
     raw_wait(2)
-    outs = tall(2)
-    down = jnp.zeros((quarter, units), F32)
-    for i in range(SIDE):
-        for kk in (0, 1):
-            down += mm_nt(
-                outs[:, (2 * i + kk) * HD : (2 * i + kk + 1) * HD], rd[i, kk]
-            )
-    ud[:, 0:units] = down.astype(BF)
+    ud[:, 0:units] = mm_nt(tall(2), deep(rd)).astype(BF)
     rs_send(1)
 
     def place(part, kk, aa, bb):
@@ -307,26 +307,30 @@
             w_send(part, k, a, bb, partner)
 
     w_sum(0)
-    p_step(UP_HOPS - lag + 2)
+    p_step(6)
     w_sum(1)
     w_pass(0)
+    p_step(7)
+    w_pass(1)
+    p_step(8)
 
     loads[2].wait()
     rows = NZ * SLOTS
     for lo in range(0, NZ, 4):
         pr = pall[lo : lo + 4].reshape(4 * SLOTS, width)
         xr = mm(pr, win_ref[...]).astype(BF)
+        xs[lo * SLOTS : (lo + 4) * SLOTS, :] = xr
         sq = xr.astype(F32)
         sq = sq * sq
         sq = sq[:, 0:128] + sq[:, 128:256]
         st[z, :, lo * SLOTS : (lo + 4) * SLOTS] = jnp.sum(jnp.transpose(sq), axis=0, keepdims=True)
-        ob[lo * SLOTS : (lo + 4) * SLOTS, :] = mm(xr, wout_ref[...])
     st_copies = []
     for j in (8, 7, 9, 6, 10, 5, 11, 4, 12, 3, 13, 2, 14, 1, 15):
         c = remote(st.at[z], st.at[z], st_s.at[j], st_r.at[z], z_peer(j))
         c.start()
         st_copies.append(c)
-    w_pass(1)
+    for lo in range(0, rows, 4 * SLOTS):
+        ob[lo : lo + 4 * SLOTS, :] = mm(xs[lo : lo + 4 * SLOTS, :], wout_ref[...])
 
     loads[3].wait()
     heads = width // HD
@@ -367,52 +371,57 @@
             for bb in range(SIDE):
                 w_wait(part, 1 - k, aa, bb)
 
-    def ffn(t):
-        d1 = (z + UP_HOPS - t) % NZ
-        d2 = (z + NZ - DOWN_HOPS + t) % NZ
-        pr = jnp.concatenate([pall[d1], pall[d2]], axis=0)
-        r = jnp.concatenate([rc[d1], rc[d2]], axis=0)
+    def ffn(dests):
+        pr = jnp.concatenate([pall[d] for d in dests], axis=0)
+        r = jnp.concatenate([rc[d] for d in dests], axis=0)
         r = jnp.concatenate([r] * (PAD // HD), axis=1)
         g = mm(pr, wf[:, 0:PAD]) * r
         u = mm(pr, wf[:, PAD : 2 * PAD]) * r
         hid = (g / (1.0 + jnp.exp(-g)) * u).astype(BF)
         o = mm_nt(hid, wf[:, 2 * PAD : 3 * PAD])
-        row1 = pl.multiple_of(d1 * SLOTS, SLOTS)
-        row2 = pl.multiple_of(d2 * SLOTS, SLOTS)
-        return (
-            o[0:SLOTS] + ob[pl.ds(row1, SLOTS), :],
-            o[SLOTS : 2 * SLOTS] + ob[pl.ds(row2, SLOTS), :],
-        )
-
-    zp_copies, zm_copies = {}, {}
-    for t in range(UP_HOPS):
-        up_val, down_val = ffn(t)
-        for h in (0, 1):
-            val = up_val[h * CUT : (h + 1) * CUT]
-            if t:
-                zp_copies[t - 1, h].wait_recv()
-                val += rzp[t - 1, h].astype(F32)
-            szp[t, h] = val.astype(BF)
-            c = remote(szp.at[t, h], rzp.at[t, h], zp_s.at[t, h], zp_r.at[t, h], above)
-            c.start()
-            zp_copies[t, h] = c
-            if t < DOWN_HOPS:
-                val = down_val[h * CUT : (h + 1) * CUT]
+        return [
+            o[i * SLOTS : (i + 1) * SLOTS] + ob[pl.ds(pl.multiple_of(d * SLOTS, SLOTS), SLOTS), :]
+            for i, d in enumerate(dests)
+        ]
+
+    chains = (
+        (8, 1, 4, above, z_peer(5), szp, rzp, zp_s, zp_r, 0),
+        (-7, -1, 3, below, z_peer(NZ - 5), szm, rzm, zm_s, zm_r, 0),
+        (4, 1, 4, above, above, szp, rzp, zp_s, zp_r, 4),
+        (-4, -1, 4, below, below, szm, rzm, zm_s, zm_r, 3),
+    )
+    z_copies = {}
+    for t in range(4):
+        live = [n for n in range(4) if t < chains[n][2]]
+        dests = [(z + NZ + chains[n][0] - chains[n][1] * t) % NZ for n in live]
+        if len(live) < 4:
+            dests.append(z)
+        vals = ffn(dests)
+        for n, val in zip(live, vals):
+            _, _, steps, target, last, out, got, ssem, rsem, base = chains[n]
+            for h in (0, 1):
+                part = val[h * CUT : (h + 1) * CUT]
                 if t:
-                    zm_copies[t - 1, h].wait_recv()
-                    val += rzm[t - 1, h].astype(F32)
-                szm[t, h] = val.astype(BF)
-                c = remote(szm.at[t, h], rzm.at[t, h], zm_s.at[t, h], zm_r.at[t, h], below)
+                    z_copies[n, t - 1, h].wait_recv()
+                    part += got[base + t - 1, h].astype(F32)
+                out[base + t, h] = part.astype(BF)
+                c = remote(
+                    out.at[base + t, h], got.at[base + t, h], ssem.at[base + t, h], rsem.at[base + t, h],
+                    last if t == steps - 1 else target,
+                )
                 c.start()
-                zm_copies[t, h] = c
-
-    vals = []
+                z_copies[n, t, h] = c
+    mine = vals[-1]
+
+    parts = []
     for h in (0, 1):
-        zm_copies[DOWN_HOPS - 1, h].wait_recv()
-        val = down_val[h * CUT : (h + 1) * CUT] + rzm[DOWN_HOPS - 1, h].astype(F32)
-        zp_copies[UP_HOPS - 1, h].wait_recv()
-        vals.append(val + rzp[UP_HOPS - 1, h].astype(F32))
-    values = jnp.concatenate(vals, axis=0)
+        val = mine[h * CUT : (h + 1) * CUT]
+        for n in (1, 3, 2, 0):
+            _, _, steps, _, _, _, got, _, _, base = chains[n]
+            z_copies[n, steps - 1, h].wait_recv()
+            val += got[base + steps - 1, h].astype(F32)
+        parts.append(val)
+    values = jnp.concatenate(parts, axis=0)
     vb = jnp.where(own, jnp.concatenate([values] * heads, axis=0), 0.0).astype(BF)
     out_ref[...] = mm(wt, vb)
 
@@ -424,20 +433,25 @@
         down_dist = (zi - z + NZ) % NZ
         for part in range(4):
 
-            @pl.when(up_dist < UP_HOPS)
+            @pl.when(jnp.logical_and(up_dist % 2 == 0, up_dist < UP_HOPS))
             def _():
-                bc_send(i, part, True).wait_send()
-
-            @pl.when(down_dist < DOWN_HOPS)
+                bc_send(i, part, True, 0).wait_send()
+                bc_send(i, part, True, 1).wait_send()
+
+            @pl.when(jnp.logical_and(down_dist % 2 == 0, down_dist < DOWN_HOPS))
             def _():
-                bc_send(i, part, False).wait_send()
+                bc_send(i, part, False, 0).wait_send()
+
+            @pl.when(jnp.logical_and(down_dist % 2 == 0, down_dist + 2 <= DOWN_HOPS))
+            def _():
+                bc_send(i, part, False, 1).wait_send()
 
     for h in (0, 1):
         for t in range(UP_HOPS):
             p_send((z + NZ - t) % NZ, h, True).wait_send()
         for t in range(DOWN_HOPS):
             p_send((z + t) % NZ, h, False).wait_send()
-    for c in (*zp_copies.values(), *zm_copies.values()):
+    for c in z_copies.values():
         c.wait_send()
 
 
@@ -473,6 +487,7 @@
             vmem((NZ, SLOTS, width), BF),
             vmem((NZ, 1, rows), F32),
             vmem((NZ, SLOTS, HD), F32),
+            vmem((rows, local), BF),
             vmem((rows, width), F32),
             vmem((UP_HOPS, 2, CUT, width), BF),
             vmem((UP_HOPS, 2, CUT, width), BF),
@@ -481,7 +496,7 @@
             vmem((SLOTS, width), F32),
             vmem((width // HD * SLOTS, nbytes), F32),
             dma((4,)), dma((7, 3)), dma((SIDE, 2, 3)), dma((3,)), dma((2,)),
-            dma((SIDE, 4)), dma((SIDE, 4)), dma((SIDE, 4)),
+            dma((SIDE, 4)), dma((SIDE, 4, 2)), dma((SIDE, 4, 2)),
             dma((2, 3)), dma((2, 3)), dma((62,)), dma((2, 2, SIDE, SIDE)),
             dma((NZ, 2)), dma((NZ, 2)), dma((NZ, 2)),
             dma((NZ,)), dma((NZ,)),

time: 107 us -> 107 us (level); the launches traced: 107 us -> 105 us
  Pallas kernels: 105 us -> 103 us
    pallas_call x1, Pallas kernels: 105 us -> 103 us  [body(): pl.pallas_call(kernel, out_shape=jax.ShapeDtypeStruct((nbytes, width), F3...]
where the time goes in v4:
time: 107 us; the launch traced here: 105 us
  Pallas kernels  103 us (96%)
  other arithmetic  2.06 us (2%)
    pallas_call x1, Pallas kernels, body(): pl.pallas_call(kernel, out_shape=jax.ShapeDtypeStruct((nbytes, width), F3...  103 us

profile of v4, /device:TPU:6, one launch (start us, length us, event | category | flops | bytes accessed | tf_op | source)
XLA Modules:
  0.0 104.8 jit_solution(15462021310072497054)
XLA Ops:
  0.0 0.0 copy-start
  0.0 102.8 %shard_map.91 = f32[192,1280]{1,0:T(8,128)} custom-call(bf16[192,1280]{1,0:T(8,128)(2,1)} %enc_hbm.1, bf16[192,1280]{1,0:T(8,128)(2,1)} %dec_hbm.1, s32[1,192]{1,0:T(1,128)} %bitcast.5, bf16[31,1280]{1,0:T(8,128)(2,1)} %keys_ref.1, bf16[1280,256]{1,0:T(8,128)(2,1)} %win_hbm.1, bf16[448,128]{1,0:T(8,128)(2,1)} %bitcast.3, bf16[448,128]{1,0:T(8,128)(2,1)} %bitcast.4, ...), custom_call_target="tpu_custom_call" | custom-call | tf_op jit(solution)/shard_map/pallas_call | solution.py:468
  102.8 0.0 copy-done
  102.8 2.1 %add_convert_fusion = bf16[192,1280]{1,0:T(8,128)(2,1)} fusion(f32[192,1280]{1,0:T(8,128)} %shard_map.91, bf16[192,1280]{1,0:T(8,128)(2,1)S(1)} %copy-done), kind=kLoop, calls=%fused_computation | loop fusion | flops 737280 | bytes 1966080 | tf_op jit(solution)/shard_map/convert_element_type | solution.py:512
Async XLA Ops:
  0.0 102.8 %copy-start = (bf16[192,1280]{1,0:T(8,128)(2,1)S(1)}, bf16[192,1280]{1,0:T(8,128)(2,1)}, u32[]{:S(2)}) copy-start(bf16[192,1280]{1,0:T(8,128)(2,1)} %dec_hbm.1) | copy-start | bytes 1474564

commit v5 on v4

--- a/solution.py
+++ b/solution.py
@@ -153,18 +153,19 @@
             c.start()
             raw_sends.append(c)
 
-    loads[0].wait()
-
-    @pl.when(hit_me)
-    def _():
-        rows = lax.broadcasted_iota(jnp.int32, (quarter, width), 0) + first_row
-        cols = lax.broadcasted_iota(jnp.int32, (quarter, width), 1)
-        pick = jnp.where(rows == cols, 1.0, 0.0).astype(BF)
-        turned = mm_nt(pick, wout_ref[...]).astype(BF)
-        for h in (0, 1):
-            bc[slot_me, 2 + h] = turned[h * eighth : (h + 1) * eighth]
-            bc_spread(slot_me, 2 + h, True)
-            bc_spread(slot_me, 2 + h, False)
+    def bc_turned():
+        loads[0].wait()
+
+        @pl.when(hit_me)
+        def _():
+            rows = lax.broadcasted_iota(jnp.int32, (quarter, width), 0) + first_row
+            cols = lax.broadcasted_iota(jnp.int32, (quarter, width), 1)
+            pick = jnp.where(rows == cols, 1.0, 0.0).astype(BF)
+            turned = mm_nt(pick, wout_ref[...]).astype(BF)
+            for h in (0, 1):
+                bc[slot_me, 2 + h] = turned[h * eighth : (h + 1) * eighth]
+                bc_spread(slot_me, 2 + h, True)
+                bc_spread(slot_me, 2 + h, False)
 
     def bc_step(t, parts):
         if not 1 <= t <= UP_HOPS // 2:
@@ -217,10 +218,15 @@
     ug[...] = jnp.zeros_like(ug)
     ud[...] = jnp.zeros_like(ud)
     p_step(0)
-    for t in range(1, 5):
-        bc_step(t, (0, 1))
-        p_step(t)
-        bc_step(t - 1, (2, 3))
+    bc_step(1, (0, 1))
+    bc_turned()
+    p_step(1)
+    bc_step(2, (0, 1))
+    p_step(2)
+    bc_step(1, (2, 3))
+    bc_step(3, (0, 1))
+    p_step(3)
+    bc_step(4, (0, 1))
 
     def raw_wait(i):
         raw_local[i].wait()
@@ -254,18 +260,6 @@
             )
             c.start()
             rs_copies[part].append(c)
-
-    raw_wait(0)
-    raw_wait(1)
-    ins = tall(0)
-    ug[:, 0:units] = mm_nt(ins, deep(rg)).astype(BF)
-    ug[:, PAD : PAD + units] = mm_nt(ins, deep(ru)).astype(BF)
-    rs_send(0)
-    bc_step(4, (2, 3))
-    p_step(5)
-    raw_wait(2)
-    ud[:, 0:units] = mm_nt(tall(2), deep(rd)).astype(BF)
-    rs_send(1)
 
     def place(part, kk, aa, bb):
         row = pl.multiple_of(kk * half + aa * quarter, 32)
@@ -306,10 +300,25 @@
                 w_send(part, k, a, bb, a_peer(i))
             w_send(part, k, a, bb, partner)
 
+    raw_wait(0)
+    raw_wait(1)
+    ins = tall(0)
+    ug[:, 0:units] = mm_nt(ins, deep(rg)).astype(BF)
+    ug[:, PAD : PAD + units] = mm_nt(ins, deep(ru)).astype(BF)
+    rs_send(0)
+    bc_step(2, (2, 3))
+    p_step(4)
+    bc_step(3, (2, 3))
     w_sum(0)
+    p_step(5)
+    bc_step(4, (2, 3))
+    raw_wait(2)
+    ud[:, 0:units] = mm_nt(tall(2), deep(rd)).astype(BF)
+    rs_send(1)
+
     p_step(6)
+    w_pass(0)
     w_sum(1)
-    w_pass(0)
     p_step(7)
     w_pass(1)
     p_step(8)

time: 107 us -> 99.4 us (0.929); the launches traced: 105 us -> 99 us
  Pallas kernels: 103 us -> 96.9 us
    pallas_call x1, Pallas kernels: 103 us -> 96.9 us  [body(): pl.pallas_call(kernel, out_shape=jax.ShapeDtypeStruct((nbytes, width), F3...]
where the time goes in v5:
time: 99.4 us; the launch traced here: 99 us
  Pallas kernels  96.9 us (97%)
  other arithmetic  2.06 us (2%)
    pallas_call x1, Pallas kernels, body(): pl.pallas_call(kernel, out_shape=jax.ShapeDtypeStruct((nbytes, width), F3...  96.9 us
    convert_element_type x1, other arithmetic, body(): return (dec_states.astype(F32) + mixed).astype(BF)  2.06 us

profile of v5, /device:TPU:6, one launch (start us, length us, event | category | flops | bytes accessed | tf_op | source)
XLA Modules:
  0.0 99.0 jit_solution(11789371631735607677)
XLA Ops:
  0.0 0.0 copy-start
  0.0 96.9 %shard_map.91 = f32[192,1280]{1,0:T(8,128)} custom-call(bf16[192,1280]{1,0:T(8,128)(2,1)} %enc_hbm.1, bf16[192,1280]{1,0:T(8,128)(2,1)} %dec_hbm.1, s32[1,192]{1,0:T(1,128)} %bitcast.5, bf16[31,1280]{1,0:T(8,128)(2,1)} %keys_ref.1, bf16[1280,256]{1,0:T(8,128)(2,1)} %win_hbm.1, bf16[448,128]{1,0:T(8,128)(2,1)} %bitcast.3, bf16[448,128]{1,0:T(8,128)(2,1)} %bitcast.4, ...), custom_call_target="tpu_custom_call" | custom-call | tf_op jit(solution)/shard_map/pallas_call | solution.py:477
  96.9 0.0 copy-done
  97.0 2.1 %add_convert_fusion = bf16[192,1280]{1,0:T(8,128)(2,1)} fusion(f32[192,1280]{1,0:T(8,128)} %shard_map.91, bf16[192,1280]{1,0:T(8,128)(2,1)S(1)} %copy-done), kind=kLoop, calls=%fused_computation | loop fusion | flops 737280 | bytes 1966080 | tf_op jit(solution)/shard_map/convert_element_type | solution.py:521
Async XLA Ops:
  0.0 96.9 %copy-start = (bf16[192,1280]{1,0:T(8,128)(2,1)S(1)}, bf16[192,1280]{1,0:T(8,128)(2,1)}, u32[]{:S(2)}) copy-start(bf16[192,1280]{1,0:T(8,128)(2,1)} %dec_hbm.1) | copy-start | bytes 1474564

commit v6 on v5

--- a/solution.py
+++ b/solution.py
@@ -225,7 +225,6 @@
     p_step(2)
     bc_step(1, (2, 3))
     bc_step(3, (0, 1))
-    p_step(3)
     bc_step(4, (0, 1))
 
     def raw_wait(i):
@@ -307,17 +306,18 @@
     ug[:, PAD : PAD + units] = mm_nt(ins, deep(ru)).astype(BF)
     rs_send(0)
     bc_step(2, (2, 3))
+    p_step(3)
+    w_sum(0)
+    bc_step(3, (2, 3))
     p_step(4)
-    bc_step(3, (2, 3))
-    w_sum(0)
-    p_step(5)
+    w_pass(0)
     bc_step(4, (2, 3))
     raw_wait(2)
     ud[:, 0:units] = mm_nt(tall(2), deep(rd)).astype(BF)
     rs_send(1)
 
+    p_step(5)
     p_step(6)
-    w_pass(0)
     w_sum(1)
     p_step(7)
     w_pass(1)
@@ -432,7 +432,7 @@
         parts.append(val)
     values = jnp.concatenate(parts, axis=0)
     vb = jnp.where(own, jnp.concatenate([values] * heads, axis=0), 0.0).astype(BF)
-    out_ref[...] = mm(wt, vb)
+    out_ref[...] = mm(wt, vb).astype(BF)
 
     for c in raw_sends + rs_copies[0] + rs_copies[1] + w_copies + st_copies:
         c.wait_send()
@@ -476,7 +476,7 @@
     here = pl.BlockSpec(memory_space=pltpu.VMEM)
     mixed = pl.pallas_call(
         kernel,
-        out_shape=jax.ShapeDtypeStruct((nbytes, width), F32),
+        out_shape=jax.ShapeDtypeStruct((nbytes, width), BF),
         in_specs=[hbm, hbm, here, here, hbm, hbm, hbm, hbm, hbm],
         out_specs=here,
         scratch_shapes=[
@@ -518,7 +518,7 @@
         enc_states, dec_states, segments.reshape(1, nbytes), patch_keys, w_in,
         w_gate.T, w_up.T, w_down, w_out,
     )
-    return (dec_states.astype(F32) + mixed).astype(BF)
+    return (dec_states.astype(F32) + mixed.astype(F32)).astype(BF)
 
 
 def solution(mesh):

time: 99.4 us -> 100 us (level)
  the two profiles are of different devices: /device:TPU:6 before, /device:TPU:32 now
where the time goes in v6:
time: 100 us; the launch traced here: 99.8 us
  Pallas kernels  97.9 us (98%)
  other arithmetic  1.92 us (2%)
    pallas_call x1, Pallas kernels, body(): pl.pallas_call(kernel, out_shape=jax.ShapeDtypeStruct((nbytes, width), BF...  97.9 us

profile of v6, /device:TPU:32, one launch (start us, length us, event | category | flops | bytes accessed | tf_op | source)
XLA Modules:
  0.0 99.8 jit_solution(1205865502561098305)
XLA Ops:
  0.0 0.0 copy-start
  0.0 97.9 %shard_map.91 = bf16[192,1280]{1,0:T(8,128)(2,1)} custom-call(bf16[192,1280]{1,0:T(8,128)(2,1)} %enc_hbm.1, bf16[192,1280]{1,0:T(8,128)(2,1)} %dec_hbm.1, s32[1,192]{1,0:T(1,128)} %bitcast.5, bf16[31,1280]{1,0:T(8,128)(2,1)} %keys_ref.1, bf16[1280,256]{1,0:T(8,128)(2,1)} %win_hbm.1, bf16[448,128]{1,0:T(8,128)(2,1)} %bitcast.3, bf16[448,128]{1,0:T(8,128)(2,1)} %bitcast.4, ...), custom_call_target="tpu_custom_call" | custom-call | tf_op jit(solution)/shard_map/pallas_call | solution.py:477
  97.9 0.0 copy-done
  97.9 1.9 %add_convert_fusion = bf16[192,1280]{1,0:T(8,128)(2,1)} fusion(bf16[192,1280]{1,0:T(8,128)(2,1)} %shard_map.91, bf16[192,1280]{1,0:T(8,128)(2,1)S(1)} %copy-done), kind=kLoop, calls=%fused_computation | loop fusion | flops 983040 | bytes 1474560 | tf_op jit(solution)/shard_map/convert_element_type | solution.py:521
Async XLA Ops:
  0.0 97.9 %copy-start = (bf16[192,1280]{1,0:T(8,128)(2,1)S(1)}, bf16[192,1280]{1,0:T(8,128)(2,1)}, u32[]{:S(2)}) copy-start(bf16[192,1280]{1,0:T(8,128)(2,1)} %dec_hbm.1) | copy-start | bytes 1474564
